TPU v7x, 32 devices: a whole 2x2x4 slice. The times are simulated.
32 devices in a mesh: groups: 2 (over x), wide: 16 (over z, y, core).
Axes of the slice: x: 2, y: 2, z: 4, core: 2. Of those that a mesh axis runs over, the one named last changes fastest.
Arguments:
- alignment_token_ids: int32 [256, 256], P(('groups', 'wide')), parts along dimension 0, may hold values from 0 to 22
- residue_index_offsets: int32 [512], P('groups'), parts along dimension 0, may hold values from 0 to 10240, as said below
- target_residue_feature: float32 [512, 256], P('groups'), parts along dimension 0, may hold values from -6 to 6
- token_embedding_table: float32 [23, 256], replicated, may hold values from -6 to 6
- attention_norm_gain: float32 [256], replicated, may hold values from 0.1 to 1.9
- query_weight: bfloat16 [256, 256], replicated, may hold values from -1 to 1
- key_weight: bfloat16 [256, 256], replicated, may hold values from -25 to 25
- value_weight: bfloat16 [256, 256], replicated, may hold values from -0.375 to 0.375
- gate_weight: bfloat16 [256, 256], replicated, may hold values from -0.375 to 0.375
- gate_offset_bias: float32 [256], replicated, may hold values from -4 to 4
- output_weight: bfloat16 [256, 256], replicated, may hold values from -0.375 to 0.375
- relative_position_table: float32 [65, 8], replicated, may hold values from -4 to 4
- product_norm_gain: float32 [256], replicated, may hold values from 0.1 to 1.9
- left_weight: bfloat16 [256, 32], replicated, may hold values from -0.375 to 0.375
- right_weight: bfloat16 [256, 32], replicated, may hold values from -0.375 to 0.375
- pair_weight: bfloat16 [1024, 128], replicated, may hold values from -0.375 to 0.375
- pair_projection_bias: float32 [128], replicated, may hold values from -3 to 3
Outputs:
- alignment_updated: float32 [256, 256, 256], P(('groups', 'wide')), parts along dimension 0
- pair: float32 [512, 256, 128], P(('groups', 'wide')), parts along dimension 0
There are 2 independent parts, one for each index of `groups`. A program takes and returns all parts, laid end to end along the dimension named above; an argument that names none is the same for every part. Nothing has to cross between parts.
Inputs may be any that keep to these rules, and one draw needn't show every extreme that they name: `residue_index_offsets`: rises by 1 from residue to residue within a chain and by more at chain breaks; the first entry is 0 and the last is 10240.
All inputs are finite; a program needn't handle non-finite values.
Results may differ from a plain program's by a relative error of at most 0.0045.
Values may be sent and summed in bfloat16 or wider, within the bound.
No kernel may reach another device: no remote copies, remote signals or barrier semaphores. Data moves between devices by JAX's collectives and lax.ppermute only.
A program may use at most 128 MiB of HBM per device.

v0:
```python
import functools
import math

import jax
import jax.numpy as jnp
from jax import lax
from jax.experimental import pallas as pl
from jax.experimental.pallas import tpu as pltpu
from jax.sharding import PartitionSpec as P


REACH = 32
LANES = 128
F32 = jnp.float32
BF16 = jnp.bfloat16


def dot(a, b, axes):
    return lax.dot_general(a, b, (axes, ((), ())), preferred_element_type=F32)


def normalize(values, gain):
    center = jnp.mean(values, axis=-1, keepdims=True)
    centred = values - center
    spread = jnp.mean(centred * centred, axis=-1, keepdims=True)
    return centred * lax.rsqrt(spread + 1e-05) * gain


def meet(place, shift, size):
    if size & (size - 1):
        return (place + shift) % size
    return place ^ shift


def nearest(devices):
    core = 2 if devices % 2 == 0 else 1
    return 2 * core if devices % (2 * core) == 0 else core


def room(shapes):
    total = 0
    for shape, dtype in shapes:
        total += math.prod(shape) * jnp.dtype(dtype).itemsize
    return total


def attention_kernel(heads, owners, outer, together, *refs):
    (
        tokens_ref,
        offsets_ref,
        target_ref,
        embed_ref,
        gain_ref,
        query_ref,
        key_ref,
        value_ref,
        gate_ref,
        gate_bias_ref,
        output_ref,
        relative_ref,
        gain_two_ref,
        left_ref,
        right_ref,
    ) = refs[:15]
    updated_ref, *rest_refs = refs[15:]
    message_refs = rest_refs[:outer]
    (
        bias_scr,
        relative_scr,
        embed_scr,
        left_scr,
        weights_scr,
        mixer_scr,
        factor_scr,
        owner_scr,
        gather_scr,
    ) = rest_refs[outer:]
    step = pl.program_id(0)
    residues, _ = target_ref.shape
    head_size = query_ref.shape[1] // heads
    packed = LANES // head_size
    groups = heads // packed
    classes = embed_ref.shape[0]
    padded = embed_scr.shape[0] // 3
    width = right_ref.shape[0]
    bins = relative_ref.shape[1]
    inner = owners // outer
    owned = residues // owners
    count = factor_scr.shape[1] // width
    slabs = owned * width // residues

    @pl.when(step == 0)
    def prepare():
        relative_scr[...] = jnp.zeros_like(relative_scr)
        relative_scr[0:heads, 0:bins] = relative_ref[...]
        table = relative_scr[...]
        row = offsets_ref[...]
        column = jnp.broadcast_to(row, (LANES, residues)).T
        for block in range(residues // LANES):
            lanes = slice(block * LANES, (block + 1) * LANES)
            start, stop = block * LANES, (block + 1) * LANES
            low = max(0, (start - REACH + 1) // 8 * 8)
            high = min(residues, -(-(stop + REACH) // 8) * 8)
            index = jnp.clip(row[:, lanes] - column[low:high], -REACH, REACH) + REACH
            for head in range(heads):
                source = jnp.broadcast_to(table[head : head + 1, :], (high - low, LANES))
                bias_scr[head, low:high, lanes] = jnp.take_along_axis(source, index, axis=1)
                if low:
                    after = table[head : head + 1, 2 * REACH : 2 * REACH + 1]
                    bias_scr[head, 0:low, lanes] = jnp.broadcast_to(after, (low, LANES))
                if high < residues:
                    before = table[head : head + 1, 0:1]
                    bias_scr[head, high:, lanes] = jnp.broadcast_to(before, (residues - high, LANES))
        embed_scr[...] = jnp.zeros_like(embed_scr)
        embed = embed_ref[...]
        high = embed.astype(BF16)
        rest = embed - high.astype(F32)
        middle = rest.astype(BF16)
        low = (rest - middle.astype(F32)).astype(BF16)
        for part, piece in enumerate((high, middle, low)):
            embed_scr[part * padded : part * padded + classes, :] = piece
        for tile in range(owned):
            left_scr[tile * width : (tile + 1) * width, :] = left_ref[...]
        gather_scr[...] = (
            lax.broadcasted_iota(jnp.int32, gather_scr.shape, 0)
            == lax.broadcasted_iota(jnp.int32, gather_scr.shape, 1) // owned
        ).astype(F32).astype(BF16)
        place = lax.broadcasted_iota(jnp.int32, (1, LANES), 1) // head_size
        for member in range(packed):
            ones = jnp.where(place == member, jnp.ones((), BF16), jnp.zeros((), BF16))
            for k in range(together):
                mixer_scr[k, member * residues : (member + 1) * residues, LANES:] = jnp.broadcast_to(
                    ones, (residues, LANES)
                )

    place = lax.broadcasted_iota(jnp.int32, (1, LANES), 1) // head_size
    blank = jnp.zeros((), BF16)
    members = range(together)
    diagonal = (
        lax.broadcasted_iota(jnp.int32, (residues, owned * width), 0) % owned
        == lax.broadcasted_iota(jnp.int32, (residues, owned * width), 1) // width
    )
    rows = [step * together + k for k in members]
    initial, normed, query, keys, values, gates = [], [], [], [], [], []
    classes_iota = lax.broadcasted_iota(jnp.int32, (padded, residues), 0)
    for k in members:
        tokens = tokens_ref[pl.ds(rows[k], 1), :]
        onehot = (classes_iota == tokens).astype(F32).astype(BF16)
        onehot = jnp.concatenate([onehot, onehot, onehot], axis=0)
        initial.append(dot(onehot, embed_scr[...], ((0,), (0,))) + target_ref[...])
    for k in members:
        normed.append(normalize(initial[k], gain_ref[...]).astype(BF16))
    for k in members:
        product = dot(normed[k], query_ref[...], ((1,), (0,)))
        query.append((product * (1.0 / head_size**0.5)).astype(BF16))
        keys.append(dot(normed[k], key_ref[...], ((1,), (0,))).astype(BF16))
        values.append(dot(normed[k], value_ref[...], ((1,), (0,))).astype(BF16))
    mixed = [[] for _ in members]
    for group in range(groups):
        lanes = slice(group * LANES, (group + 1) * LANES)
        for member in range(packed):
            mine = place == member
            columns = slice(member * residues, (member + 1) * residues)
            for k in members:
                one_query = jnp.where(mine, query[k][:, lanes], blank)
                scores = dot(one_query, keys[k][:, lanes], ((1,), (1,)))
                scores = scores + bias_scr[group * packed + member]
                expo = jnp.exp(scores - jnp.max(scores, axis=-1, keepdims=True))
                weights_scr[k, :, columns] = expo.astype(BF16)
                mixer_scr[k, columns, 0:LANES] = jnp.where(mine, values[k][:, lanes], blank)
        for k in members:
            both = dot(weights_scr[k], mixer_scr[k], ((1,), (0,)))
            mixed[k].append(both[:, :LANES] / both[:, LANES:])
    for k in members:
        gates.append(jax.nn.sigmoid(dot(normed[k], gate_ref[...], ((1,), (0,))) + gate_bias_ref[...]))
    for k in members:
        whole = (jnp.concatenate(mixed[k], axis=1) * gates[k]).astype(BF16)
        updated = initial[k] + dot(whole, output_ref[...], ((1,), (0,)))
        updated_ref[k] = updated
        normed_two = normalize(updated, gain_two_ref[...])
        narrow = normed_two.astype(BF16)
        spread_left = dot(narrow, left_scr[...], ((1,), (1,)))
        spread_left = jnp.where(diagonal, spread_left, 0.0).astype(BF16)
        folded = dot(gather_scr[...], spread_left, ((1,), (0,)))
        for tile in range(owned * width // LANES):
            lanes = slice(tile * LANES, (tile + 1) * LANES)
            owner_scr[tile, pl.ds(rows[k], owners, stride=count), :] = folded[:, lanes]
        right = dot(right_ref[...], narrow, ((1,), (1,)))
        for tile in range(residues // LANES):
            lanes = slice(tile * LANES, (tile + 1) * LANES)
            factor_scr[tile, pl.ds(rows[k], width, stride=count), :] = right[:, lanes]

    @pl.when(step == pl.num_programs(0) - 1)
    def finish():
        right = jnp.concatenate([factor_scr[t] for t in range(residues // LANES)], axis=1)
        right = right.astype(BF16).reshape(width, count, residues)
        mine = lax.axis_index("wide") // inner
        per = residues // LANES
        for shift, message_ref in enumerate(message_refs):
            target = meet(mine, shift, outer) * inner
            message_ref[0:width] = right
            for k in range(inner):
                start = pl.multiple_of((target + k) * count, count)
                for slab in range(slabs):
                    block = [owner_scr[slab * per + t, pl.ds(start, count), :] for t in range(per)]
                    message_ref[width + k * slabs + slab] = jnp.concatenate(block, axis=1).astype(BF16)


def attention(operands, heads, owners, outer):
    tokens, _, target, embed, _, query_weight = operands[:6]
    _, right_weight = operands[13:15]
    count, residues = tokens.shape
    features = target.shape[1]
    head_size = query_weight.shape[1] // heads
    packed = LANES // head_size
    width = right_weight.shape[0]
    owned = residues // owners
    padded = -(-embed.shape[0] // 32) * 32
    together = 2 if count % 2 == 0 else 1
    whole = lambda x: pl.BlockSpec(x.shape, lambda s, n=x.ndim: (0,) * n)
    slabs = owned * width // residues
    message = (width + owners // outer * slabs, count, residues)
    outs = (jax.ShapeDtypeStruct((count, residues, features), F32),) + (
        jax.ShapeDtypeStruct(message, BF16),
    ) * outer
    scratch = [
        ((heads, residues, residues), F32),
        ((heads, LANES), F32),
        ((3 * padded, features), BF16),
        ((owned * width, features), BF16),
        ((together, residues, packed * residues), BF16),
        ((together, packed * residues, 2 * LANES), BF16),
        ((residues // LANES, width * count, LANES), F32),
        ((owned * width // LANES, owners * count, LANES), F32),
        ((owners, residues), BF16),
    ]
    return pl.pallas_call(
        functools.partial(attention_kernel, heads, owners, outer, together),
        grid=(count // together,),
        in_specs=[whole(x) for x in operands],
        out_specs=(pl.BlockSpec((together, residues, features), lambda s: (s, 0, 0)),)
        + tuple(whole(x) for x in outs[1:]),
        out_shape=outs,
        scratch_shapes=[pltpu.VMEM(shape, dtype) for shape, dtype in scratch],
        cost_estimate=pl.CostEstimate(
            flops=count * residues * (8 * features * features + 8 * heads * residues * LANES),
            transcendentals=count * heads * residues * residues,
            bytes_accessed=4 * count * residues * features,
        ),
        name="attention",
    )(*operands)


def spread(messages, devices):
    outer = len(messages)
    inner = devices // outer
    core = 2 if inner % 2 == 0 else 1

    def move(piece, target):
        return lax.ppermute(piece, "wide", [(d, target(d)) for d in range(devices)])

    pieces = [messages[0]] + [
        move(message, lambda d, k=shift: meet(d // inner, k, outer) * inner + d % inner)
        for shift, message in enumerate(messages)
        if shift
    ]
    for axis, stride in ((inner // core, core), (core, 1)):
        pieces = pieces + [
            move(piece, lambda d, k=shift: d + ((d // stride + k) % axis - d // stride % axis) * stride)
            for shift in range(1, axis)
            for piece in pieces
        ]
    return pieces


def order_kernel(weight_ref, own_ref, out_ref, kept_ref, wide_scr, sem):
    width = round(weight_ref.shape[0] ** 0.5)
    copy = pltpu.make_async_copy(own_ref, kept_ref, sem)
    copy.start()
    wide_scr[...] = weight_ref[...].astype(F32)
    for e in range(width):
        out_ref[:, e * width : (e + 1) * width] = wide_scr[pl.ds(e, width, stride=width), :].T.astype(BF16)
    copy.wait()


def ordered(weight, own):
    shape = weight.shape[::-1]
    return pl.pallas_call(
        order_kernel,
        in_specs=[pl.BlockSpec(weight.shape, lambda: (0, 0)), pl.BlockSpec(memory_space=pl.ANY)],
        out_shape=(jax.ShapeDtypeStruct(shape, BF16), jax.ShapeDtypeStruct(own.shape, own.dtype)),
        scratch_shapes=[pltpu.VMEM(weight.shape, F32), pltpu.SemaphoreType.DMA],
        compiler_params=pltpu.CompilerParams(vmem_limit_bytes=8 * 2**20),
        cost_estimate=pl.CostEstimate(flops=0, transcendentals=0, bytes_accessed=4 * math.prod(shape)),
        name="order",
    )(weight, own)


def pair_kernel(count, halves, inner, weight_ref, bias_ref, *rest_refs):
    pieces = len(rest_refs) - 6
    piece_refs = rest_refs[:pieces]
    out_ref, right_scr, left_scr, flat_scr, outer_scr, sems = rest_refs[pieces:]
    groups, depth, residues = right_scr.shape
    height = halves * count
    width = groups * halves
    block = out_ref.shape[0]
    half = flat_scr.shape[1] // halves
    slabs = left_scr.shape[0]

    @pl.when(pl.program_id(0) == 0)
    def prepare():
        mine = lax.rem(lax.axis_index("wide"), inner) * slabs + groups
        copies = []
        for number, piece_ref in enumerate(piece_refs):
            rows = pl.ds(number * height, height)
            copies.append(
                pltpu.make_async_copy(
                    piece_ref.at[pl.ds(mine, slabs)], left_scr.at[:, rows], sems.at[0, number]
                )
            )
            copies.append(
                pltpu.make_async_copy(
                    piece_ref.at[pl.ds(0, groups)], right_scr.at[:, rows], sems.at[1, number]
                )
            )
        for copy in copies:
            copy.start()
        for copy in copies[0::2]:
            copy.wait()
        left = jnp.concatenate([left_scr[slab] for slab in range(slabs)], axis=1)[:, 0:half].astype(F32)
        member = lax.broadcasted_iota(jnp.int32, (depth, 1), 0) % height // count
        for e in range(halves):
            for h in range(halves):
                moved = left
                if e != h:
                    moved = pltpu.roll(left.reshape(pieces, height, half), (e - h) % halves * count, 1)
                    moved = moved.reshape(depth, half)
                moved = jnp.where(member == e, moved, 0.0)
                flat_scr[e, h * half : (h + 1) * half, :] = moved.T.astype(BF16)
        for copy in copies[1::2]:
            copy.wait()

    rows = block * width
    start = pl.multiple_of(pl.program_id(0) * rows, rows)
    for group in range(groups):
        for e in range(halves):
            product = dot(flat_scr[e, pl.ds(start, rows), :], right_scr[group], ((1,), (0,))).astype(BF16)
            place = (group * halves + e) * width
            outer_scr[:, place : place + width, :] = product.reshape(block, width, residues)
    total = float(pieces * count)
    for i in range(block):
        projected = dot(weight_ref[...], outer_scr[i], ((1,), (0,)))
        out_ref[i] = projected.T * (1.0 / total) + bias_ref[...]


def pair_features(pieces, weight, bias, count, inner, owned, blocks):
    slabs, height, residues = pieces[0].shape
    halves = height // count
    width = round(weight.shape[1] ** 0.5)
    groups = width // halves
    slabs = (slabs - groups) // inner
    depth = len(pieces) * height
    channels = weight.shape[0]
    block = owned // blocks
    scratch = [
        ((groups, depth, residues), BF16),
        ((slabs, depth, residues), BF16),
        ((halves, owned * width, depth), BF16),
        ((block, width * width, residues), BF16),
    ]
    used = room(scratch) + 2 * room([(weight.shape, BF16), ((block, residues, channels), F32)])
    return pl.pallas_call(
        functools.partial(pair_kernel, count, halves, inner),
        grid=(blocks,),
        in_specs=[
            pl.BlockSpec(weight.shape, lambda i: (0, 0)),
            pl.BlockSpec((1, channels), lambda i: (0, 0)),
        ]
        + [pl.BlockSpec(memory_space=pl.ANY)] * len(pieces),
        out_specs=pl.BlockSpec((block, residues, channels), lambda i: (i, 0, 0)),
        out_shape=jax.ShapeDtypeStruct((owned, residues, channels), F32),
        scratch_shapes=[pltpu.VMEM(shape, dtype) for shape, dtype in scratch]
        + [pltpu.SemaphoreType.DMA((2, len(pieces)))],
        compiler_params=pltpu.CompilerParams(vmem_limit_bytes=used + 12 * 2**20),
        name="pair",
    )(weight, bias.reshape(1, -1), *pieces)


def shards(
    alignment_token_ids,
    residue_index_offsets,
    target_residue_feature,
    token_embedding_table,
    attention_norm_gain,
    query_weight,
    key_weight,
    value_weight,
    gate_weight,
    gate_offset_bias,
    output_weight,
    relative_position_table,
    product_norm_gain,
    left_weight,
    right_weight,
    pair_weight,
    pair_projection_bias,
):
    devices = lax.axis_size("wide")
    inner = nearest(devices)
    sequences, residues = alignment_token_ids.shape
    operands = (
        alignment_token_ids,
        residue_index_offsets.reshape(1, -1),
        target_residue_feature,
        token_embedding_table,
        attention_norm_gain.reshape(1, -1),
        query_weight,
        key_weight,
        value_weight,
        gate_weight,
        gate_offset_bias.reshape(1, -1),
        output_weight,
        relative_position_table.T,
        product_norm_gain.reshape(1, -1),
        left_weight.T,
        right_weight.T,
    )
    heads = relative_position_table.shape[1]
    updated, *messages = attention(operands, heads, devices, devices // inner)
    pieces = spread(messages, devices)
    weight, pieces[0] = ordered(pair_weight, messages[0])
    pair = pair_features(
        pieces,
        weight,
        pair_projection_bias,
        sequences,
        inner,
        residues // devices,
        2,
    )
    return (updated, pair)


def solution(mesh):
    placed = (P(("groups", "wide"), None), P("groups"), P("groups", None)) + (P(),) * 14
    return jax.shard_map(
        shards,
        mesh=mesh,
        in_specs=placed,
        out_specs=(P(("groups", "wide"), None, None), P(("groups", "wide"), None, None)),
        check_vma=False,
    )
```

profile of v0, /device:TPU:0, one launch (start us, length us, event | category | flops | bytes accessed | tf_op | source)
XLA Modules:
  0.0 56.0 jit_solution(6111564591844834734)
XLA Ops:
  0.7 17.1 %attention.1 = (f32[8,256,256]{2,1,0:T(8,128)}, bf16[40,8,256]{2,1,0:T(8,128)(2,1)}, bf16[40,8,256]{2,1,0:T(8,128)(2,1)}, bf16[40,8,256]{2,1,0:T(8,128)(2,1)}, bf16[40,8,256]{2,1,0:T(8,128)(2,1)}) custom-call(s32[8,256]{1,0:T(8,128)} %refs_0_.1, s32[1,256]{1,0:T(1,128)} %bitcast.12, f32[256,256]{1,0:T(8,128)} %refs_2_.1, f32[23,256]{1,0:T(8,128)} %refs_3_.1, ...), custom_call_target="tpu_custom_call" | custom-call | flops 5368709120 | bytes 2097152 | tf_op jit(solution)/shard_map/attention/pallas_call | solution.py:237
  17.7 3.1 %collective-permute-start = (bf16[40,8,256]{2,1,0:T(8,128)(2,1)}, bf16[40,8,256]{2,1,0:T(8,128)(2,1)S(1)}, u32[]{:S(2)}, u32[]{:S(2)}) collective-permute-start(bf16[40,8,256]{2,1,0:T(8,128)(2,1)} %get-tuple-element.13), channel_id=1, source_target_pairs={{0,4},{1,5},{2,6},{3,7},{4,0},{5,1},{6,2},{7,3},{8,12},{9,13},{10,... | collective-permute-start | bytes 491528 | tf_op jit(solution)/shard_map/ppermute | solution.py:260
  20.8 2.6 %collective-permute-start.1 = (bf16[40,8,256]{2,1,0:T(8,128)(2,1)}, bf16[40,8,256]{2,1,0:T(8,128)(2,1)S(1)}, u32[]{:S(2)}, u32[]{:S(2)}) collective-permute-start(bf16[40,8,256]{2,1,0:T(8,128)(2,1)} %get-tuple-element.14), channel_id=1, source_target_pairs={{0,8},{1,9},{2,10},{3,11},{4,12},{5,13},{6,14},{7,15},{8,0},{9,1},... | collective-permute-start | bytes 491528 | tf_op jit(solution)/shard_map/ppermute | solution.py:260
  23.4 0.0 collective-permute-start.2
  23.4 0.0 collective-permute-start.7
  23.4 1.7 %collective-permute-start.3 = (bf16[40,8,256]{2,1,0:T(8,128)(2,1)}, bf16[40,8,256]{2,1,0:T(8,128)(2,1)S(1)}, u32[]{:S(2)}, u32[]{:S(2)}) collective-permute-start(bf16[40,8,256]{2,1,0:T(8,128)(2,1)} %get-tuple-element.10.own_ref), channel_id=1, source_target_pairs={{0,2},{1,3},{2,0},{3,1},{4,6},{5,7},{6,4},{7,5},{8,10},{9,11},{10,... | collective-permute-start | bytes 491528 | tf_op jit(solution)/shard_map/ppermute | solution.py:260
  25.2 2.6 %collective-permute-done.rest_refs_1_ = bf16[40,8,256]{2,1,0:T(8,128)(2,1)S(1)} collective-permute-done((bf16[40,8,256]{2,1,0:T(8,128)(2,1)}, bf16[40,8,256]{2,1,0:T(8,128)(2,1)S(1)}, u32[]{:S(2)}, u32[]{:S(2)}) %collective-permute-start) | collective-permute-done | bytes 163872 | tf_op jit(solution)/shard_map/ppermute | solution.py:260
  27.8 8.3 %collective-permute-done.1.rest_refs_2_ = bf16[40,8,256]{2,1,0:T(8,128)(2,1)S(1)} collective-permute-done((bf16[40,8,256]{2,1,0:T(8,128)(2,1)}, bf16[40,8,256]{2,1,0:T(8,128)(2,1)S(1)}, u32[]{:S(2)}, u32[]{:S(2)}) %collective-permute-start.1) | collective-permute-done | bytes 163872 | tf_op jit(solution)/shard_map/ppermute | solution.py:260
  36.0 1.5 %collective-permute-start.4 = (bf16[40,8,256]{2,1,0:T(8,128)(2,1)S(1)}, bf16[40,8,256]{2,1,0:T(8,128)(2,1)S(1)}, u32[]{:S(2)}, u32[]{:S(2)}) collective-permute-start(bf16[40,8,256]{2,1,0:T(8,128)(2,1)S(1)} %collective-permute-done.rest_refs_1_), channel_id=1, source_target_pairs={{0,2},{1,3},{2,0},{3,1},{4,6},{5,7},{6,4},{7,5},{8,10},{9,11},{10,... | collective-permute-start | bytes 491528 | tf_op jit(solution)/shard_map/ppermute | solution.py:260
  37.6 0.6 %collective-permute-start.5 = (bf16[40,8,256]{2,1,0:T(8,128)(2,1)S(1)}, bf16[40,8,256]{2,1,0:T(8,128)(2,1)S(1)}, u32[]{:S(2)}, u32[]{:S(2)}) collective-permute-start(bf16[40,8,256]{2,1,0:T(8,128)(2,1)S(1)} %collective-permute-done.1.rest_refs_2_), channel_id=1, source_target_pairs={{0,2},{1,3},{2,0},{3,1},{4,6},{5,7},{6,4},{7,5},{8,10},{9,11},{10,... | collective-permute-start | bytes 491528 | tf_op jit(solution)/shard_map/ppermute | solution.py:260
  38.1 1.5 %collective-permute-start.6 = (bf16[40,8,256]{2,1,0:T(8,128)(2,1)S(1)}, bf16[40,8,256]{2,1,0:T(8,128)(2,1)S(1)}, u32[]{:S(2)}, u32[]{:S(2)}) collective-permute-start(bf16[40,8,256]{2,1,0:T(8,128)(2,1)S(1)} %collective-permute-done.2.rest_refs_3_), channel_id=1, source_target_pairs={{0,2},{1,3},{2,0},{3,1},{4,6},{5,7},{6,4},{7,5},{8,10},{9,11},{10,... | collective-permute-start | bytes 491528 | tf_op jit(solution)/shard_map/ppermute | solution.py:260
  39.7 2.4 %collective-permute-done.4.rest_refs_5_ = bf16[40,8,256]{2,1,0:T(8,128)(2,1)S(1)} collective-permute-done((bf16[40,8,256]{2,1,0:T(8,128)(2,1)S(1)}, bf16[40,8,256]{2,1,0:T(8,128)(2,1)S(1)}, u32[]{:S(2)}, u32[]{:S(2)}) %collective-permute-start.4) | collective-permute-done | bytes 163872 | tf_op jit(solution)/shard_map/ppermute | solution.py:260
  42.1 0.5 collective-permute-start.12
  42.6 3.0 %collective-permute-done.5.rest_refs_6_ = bf16[40,8,256]{2,1,0:T(8,128)(2,1)S(1)} collective-permute-done((bf16[40,8,256]{2,1,0:T(8,128)(2,1)S(1)}, bf16[40,8,256]{2,1,0:T(8,128)(2,1)S(1)}, u32[]{:S(2)}, u32[]{:S(2)}) %collective-permute-start.5) | collective-permute-done | bytes 163872 | tf_op jit(solution)/shard_map/ppermute | solution.py:260
  45.6 0.0 collective-permute-start.13
  45.6 2.8 %collective-permute-done.6.rest_refs_7_ = bf16[40,8,256]{2,1,0:T(8,128)(2,1)S(1)} collective-permute-done((bf16[40,8,256]{2,1,0:T(8,128)(2,1)S(1)}, bf16[40,8,256]{2,1,0:T(8,128)(2,1)S(1)}, u32[]{:S(2)}, u32[]{:S(2)}) %collective-permute-start.6) | collective-permute-done | bytes 163872 | tf_op jit(solution)/shard_map/ppermute | solution.py:260
  48.4 0.0 collective-permute-start.14
  48.4 0.9 %copy-done.1 = bf16[40,8,256]{2,1,0:T(8,128)(2,1)S(1)} copy-done((bf16[40,8,256]{2,1,0:T(8,128)(2,1)S(1)}, bf16[40,8,256]{2,1,0:T(8,128)(2,1)}, u32[]{:S(2)}) %copy-start.1) | copy-done | bytes 163864
  49.3 1.1 %order.1 = (bf16[128,1024]{1,0:T(8,128)(2,1)S(1)}, bf16[40,8,256]{2,1,0:T(8,128)(2,1)S(1)}) custom-call(bf16[1024,128]{1,0:T(8,128)(2,1)S(1)} %copy-done, bf16[40,8,256]{2,1,0:T(8,128)(2,1)S(1)} %copy-done.1), custom_call_target="tpu_custom_call" | custom-call | bytes 524288 | tf_op jit(solution)/shard_map/order/pallas_call | solution.py:288
  50.4 0.0 collective-permute-done.10.rest_refs_11_
  50.4 0.0 collective-permute-done.11.rest_refs_12_
  50.4 0.0 collective-permute-done.13.rest_refs_14_
  50.4 0.0 collective-permute-done.14.rest_refs_15_
  50.4 5.6 %pair.1 = f32[16,256,128]{2,1,0:T(8,128)} custom-call(bf16[128,1024]{1,0:T(8,128)(2,1)S(1)} %get-tuple-element.11.weight_ref, f32[1,128]{1,0:T(1,128)S(1)} %bitcast.8, bf16[40,8,256]{2,1,0:T(8,128)(2,1)S(1)} %get-tuple-element.12.rest_refs_0_, bf16[40,8,256]{2,1,0:T(8,128)(2,1)S(1)} %collective-permute-done.rest_refs_1_, ...), custom_call_target="tpu_custom_call" | custom-call | tf_op jit(solution)/shard_map/pair/pallas_call | solution.py:372
  (15 shorter events, 0.0 us)
Async XLA Ops:
  0.6 47.8 %copy-start = (bf16[1024,128]{1,0:T(8,128)(2,1)S(1)}, bf16[1024,128]{1,0:T(8,128)(2,1)}, u32[]{:S(2)}) copy-start(bf16[1024,128]{1,0:T(8,128)(2,1)} %weight_ref.1) | copy-start | bytes 786436
  0.6 49.8 %copy-start.2 = (f32[128]{0:T(128)S(1)}, f32[128]{0:T(128)}, u32[]{:S(2)}) copy-start(f32[128]{0:T(128)} %param.33) | copy-start | bytes 1540
  17.7 10.0 %collective-permute-start = (bf16[40,8,256]{2,1,0:T(8,128)(2,1)}, bf16[40,8,256]{2,1,0:T(8,128)(2,1)S(1)}, u32[]{:S(2)}, u32[]{:S(2)}) collective-permute-start(bf16[40,8,256]{2,1,0:T(8,128)(2,1)} %get-tuple-element.13), channel_id=1, source_target_pairs={{0,4},{1,5},{2,6},{3,7},{4,0},{5,1},{6,2},{7,3},{8,12},{9,13},{10,... | collective-permute-start | bytes 491528 | tf_op jit(solution)/shard_map/ppermute | solution.py:260
  20.8 15.2 %collective-permute-start.1 = (bf16[40,8,256]{2,1,0:T(8,128)(2,1)}, bf16[40,8,256]{2,1,0:T(8,128)(2,1)S(1)}, u32[]{:S(2)}, u32[]{:S(2)}) collective-permute-start(bf16[40,8,256]{2,1,0:T(8,128)(2,1)} %get-tuple-element.14), channel_id=1, source_target_pairs={{0,8},{1,9},{2,10},{3,11},{4,12},{5,13},{6,14},{7,15},{8,0},{9,1},... | collective-permute-start | bytes 491528 | tf_op jit(solution)/shard_map/ppermute | solution.py:260
  23.4 14.1 %collective-permute-start.2 = (bf16[40,8,256]{2,1,0:T(8,128)(2,1)}, bf16[40,8,256]{2,1,0:T(8,128)(2,1)S(1)}, u32[]{:S(2)}, u32[]{:S(2)}) collective-permute-start(bf16[40,8,256]{2,1,0:T(8,128)(2,1)} %get-tuple-element.15), channel_id=1, source_target_pairs={{0,12},{1,13},{2,14},{3,15},{4,8},{5,9},{6,10},{7,11},{8,4},{9,5},... | collective-permute-start | bytes 491528 | tf_op jit(solution)/shard_map/ppermute | solution.py:260
  23.4 14.1 %collective-permute-start.7 = (bf16[40,8,256]{2,1,0:T(8,128)(2,1)}, bf16[40,8,256]{2,1,0:T(8,128)(2,1)S(1)}, u32[]{:S(2)}, u32[]{:S(2)}) collective-permute-start(bf16[40,8,256]{2,1,0:T(8,128)(2,1)} %get-tuple-element.10.own_ref), channel_id=1, source_target_pairs={{0,1},{1,0},{2,3},{3,2},{4,5},{5,4},{6,7},{7,6},{8,9},{9,8},{10,11... | collective-permute-start | bytes 491528 | tf_op jit(solution)/shard_map/ppermute | solution.py:260
  23.4 14.7 %collective-permute-start.3 = (bf16[40,8,256]{2,1,0:T(8,128)(2,1)}, bf16[40,8,256]{2,1,0:T(8,128)(2,1)S(1)}, u32[]{:S(2)}, u32[]{:S(2)}) collective-permute-start(bf16[40,8,256]{2,1,0:T(8,128)(2,1)} %get-tuple-element.10.own_ref), channel_id=1, source_target_pairs={{0,2},{1,3},{2,0},{3,1},{4,6},{5,7},{6,4},{7,5},{8,10},{9,11},{10,... | collective-permute-start | bytes 491528 | tf_op jit(solution)/shard_map/ppermute | solution.py:260
  27.8 11.9 %collective-permute-start.8 = (bf16[40,8,256]{2,1,0:T(8,128)(2,1)S(1)}, bf16[40,8,256]{2,1,0:T(8,128)(2,1)S(1)}, u32[]{:S(2)}, u32[]{:S(2)}) collective-permute-start(bf16[40,8,256]{2,1,0:T(8,128)(2,1)S(1)} %collective-permute-done.rest_refs_1_), channel_id=1, source_target_pairs={{0,1},{1,0},{2,3},{3,2},{4,5},{5,4},{6,7},{7,6},{8,9},{9,8},{10,11... | collective-permute-start | bytes 491528 | tf_op jit(solution)/shard_map/ppermute | solution.py:260
  36.0 6.1 %collective-permute-start.4 = (bf16[40,8,256]{2,1,0:T(8,128)(2,1)S(1)}, bf16[40,8,256]{2,1,0:T(8,128)(2,1)S(1)}, u32[]{:S(2)}, u32[]{:S(2)}) collective-permute-start(bf16[40,8,256]{2,1,0:T(8,128)(2,1)S(1)} %collective-permute-done.rest_refs_1_), channel_id=1, source_target_pairs={{0,2},{1,3},{2,0},{3,1},{4,6},{5,7},{6,4},{7,5},{8,10},{9,11},{10,... | collective-permute-start | bytes 491528 | tf_op jit(solution)/shard_map/ppermute | solution.py:260
  37.6 4.5 %collective-permute-start.9 = (bf16[40,8,256]{2,1,0:T(8,128)(2,1)S(1)}, bf16[40,8,256]{2,1,0:T(8,128)(2,1)S(1)}, u32[]{:S(2)}, u32[]{:S(2)}) collective-permute-start(bf16[40,8,256]{2,1,0:T(8,128)(2,1)S(1)} %collective-permute-done.1.rest_refs_2_), channel_id=1, source_target_pairs={{0,1},{1,0},{2,3},{3,2},{4,5},{5,4},{6,7},{7,6},{8,9},{9,8},{10,11... | collective-permute-start | bytes 491528 | tf_op jit(solution)/shard_map/ppermute | solution.py:260
  37.6 8.0 %collective-permute-start.5 = (bf16[40,8,256]{2,1,0:T(8,128)(2,1)S(1)}, bf16[40,8,256]{2,1,0:T(8,128)(2,1)S(1)}, u32[]{:S(2)}, u32[]{:S(2)}) collective-permute-start(bf16[40,8,256]{2,1,0:T(8,128)(2,1)S(1)} %collective-permute-done.1.rest_refs_2_), channel_id=1, source_target_pairs={{0,2},{1,3},{2,0},{3,1},{4,6},{5,7},{6,4},{7,5},{8,10},{9,11},{10,... | collective-permute-start | bytes 491528 | tf_op jit(solution)/shard_map/ppermute | solution.py:260
  38.1 10.2 %collective-permute-start.6 = (bf16[40,8,256]{2,1,0:T(8,128)(2,1)S(1)}, bf16[40,8,256]{2,1,0:T(8,128)(2,1)S(1)}, u32[]{:S(2)}, u32[]{:S(2)}) collective-permute-start(bf16[40,8,256]{2,1,0:T(8,128)(2,1)S(1)} %collective-permute-done.2.rest_refs_3_), channel_id=1, source_target_pairs={{0,2},{1,3},{2,0},{3,1},{4,6},{5,7},{6,4},{7,5},{8,10},{9,11},{10,... | collective-permute-start | bytes 491528 | tf_op jit(solution)/shard_map/ppermute | solution.py:260
  39.7 10.7 %collective-permute-start.10 = (bf16[40,8,256]{2,1,0:T(8,128)(2,1)S(1)}, bf16[40,8,256]{2,1,0:T(8,128)(2,1)S(1)}, u32[]{:S(2)}, u32[]{:S(2)}) collective-permute-start(bf16[40,8,256]{2,1,0:T(8,128)(2,1)S(1)} %collective-permute-done.2.rest_refs_3_), channel_id=1, source_target_pairs={{0,1},{1,0},{2,3},{3,2},{4,5},{5,4},{6,7},{7,6},{8,9},{9,8},{10,11... | collective-permute-start | bytes 491528 | tf_op jit(solution)/shard_map/ppermute | solution.py:260
  42.1 8.3 %collective-permute-start.11 = (bf16[40,8,256]{2,1,0:T(8,128)(2,1)S(1)}, bf16[40,8,256]{2,1,0:T(8,128)(2,1)S(1)}, u32[]{:S(2)}, u32[]{:S(2)}) collective-permute-start(bf16[40,8,256]{2,1,0:T(8,128)(2,1)S(1)} %collective-permute-done.3.rest_refs_4_), channel_id=1, source_target_pairs={{0,1},{1,0},{2,3},{3,2},{4,5},{5,4},{6,7},{7,6},{8,9},{9,8},{10,11... | collective-permute-start | bytes 491528 | tf_op jit(solution)/shard_map/ppermute | solution.py:260
  42.1 8.3 %collective-permute-start.12 = (bf16[40,8,256]{2,1,0:T(8,128)(2,1)S(1)}, bf16[40,8,256]{2,1,0:T(8,128)(2,1)S(1)}, u32[]{:S(2)}, u32[]{:S(2)}) collective-permute-start(bf16[40,8,256]{2,1,0:T(8,128)(2,1)S(1)} %collective-permute-done.4.rest_refs_5_), channel_id=1, source_target_pairs={{0,1},{1,0},{2,3},{3,2},{4,5},{5,4},{6,7},{7,6},{8,9},{9,8},{10,11... | collective-permute-start | bytes 491528 | tf_op jit(solution)/shard_map/ppermute | solution.py:260
  45.6 4.8 %collective-permute-start.13 = (bf16[40,8,256]{2,1,0:T(8,128)(2,1)S(1)}, bf16[40,8,256]{2,1,0:T(8,128)(2,1)S(1)}, u32[]{:S(2)}, u32[]{:S(2)}) collective-permute-start(bf16[40,8,256]{2,1,0:T(8,128)(2,1)S(1)} %collective-permute-done.5.rest_refs_6_), channel_id=1, source_target_pairs={{0,1},{1,0},{2,3},{3,2},{4,5},{5,4},{6,7},{7,6},{8,9},{9,8},{10,11... | collective-permute-start | bytes 491528 | tf_op jit(solution)/shard_map/ppermute | solution.py:260
  48.4 2.0 %collective-permute-start.14 = (bf16[40,8,256]{2,1,0:T(8,128)(2,1)S(1)}, bf16[40,8,256]{2,1,0:T(8,128)(2,1)S(1)}, u32[]{:S(2)}, u32[]{:S(2)}) collective-permute-start(bf16[40,8,256]{2,1,0:T(8,128)(2,1)S(1)} %collective-permute-done.6.rest_refs_7_), channel_id=1, source_target_pairs={{0,1},{1,0},{2,3},{3,2},{4,5},{5,4},{6,7},{7,6},{8,9},{9,8},{10,11... | collective-permute-start | bytes 491528 | tf_op jit(solution)/shard_map/ppermute | solution.py:260
  48.4 0.9 %copy-start.1 = (bf16[40,8,256]{2,1,0:T(8,128)(2,1)S(1)}, bf16[40,8,256]{2,1,0:T(8,128)(2,1)}, u32[]{:S(2)}) copy-start(bf16[40,8,256]{2,1,0:T(8,128)(2,1)} %get-tuple-element.10.own_ref) | copy-start | bytes 491524
where the time goes:
time: 56.2 us; the launch traced here: 56 us
  Pallas kernels  23.7 us (42%)
  waiting for transfers between devices  19.1 us (34%)
  starting transfers between devices  11.6 us (21%)
  local copies, waits for them, and re-layouts  0.92 us (2%)
  between operations  0.73 us (1%)
    ppermute x15, waiting for transfers between devices, move(): return lax.ppermute(piece, 'wide', [(d, target(d)) for d in range(devices)])  19.1 us
    pallas_call x1, Pallas kernels, attention(): pl.pallas_call(functools.partial(attention_kernel, heads, owners, outer,...  17.1 us
    ppermute x15, starting transfers between devices, move(): return lax.ppermute(piece, 'wide', [(d, target(d)) for d in range(devices)])  11.6 us
    pallas_call x1, Pallas kernels, pair_features(): pl.pallas_call(functools.partial(pair_kernel, count, halves, inner), grid...  5.6 us
  transfers between devices with their start and end apart: 15, of which 5 were waited for; matrix products, arithmetic and copies ran while one was open for 0% of the time, Pallas kernels for 2%

commit v1 on v0

--- a/solution.py
+++ b/solution.py
@@ -74,9 +74,11 @@
         factor_scr,
         owner_scr,
         gather_scr,
+        narrow_scr,
+        sorted_scr,
     ) = rest_refs[outer:]
     step = pl.program_id(0)
-    residues, _ = target_ref.shape
+    residues, features = target_ref.shape
     head_size = query_ref.shape[1] // heads
     packed = LANES // head_size
     groups = heads // packed
@@ -101,10 +103,13 @@
             start, stop = block * LANES, (block + 1) * LANES
             low = max(0, (start - REACH + 1) // 8 * 8)
             high = min(residues, -(-(stop + REACH) // 8) * 8)
-            index = jnp.clip(row[:, lanes] - column[low:high], -REACH, REACH) + REACH
+            for tile in range(low, high, 8):
+                rows = slice(tile, tile + 8)
+                index = jnp.clip(row[:, lanes] - column[rows], -REACH, REACH) + REACH
+                for head in range(heads):
+                    source = jnp.broadcast_to(table[head : head + 1, :], (8, LANES))
+                    bias_scr[head, rows, lanes] = jnp.take_along_axis(source, index, axis=1)
             for head in range(heads):
-                source = jnp.broadcast_to(table[head : head + 1, :], (high - low, LANES))
-                bias_scr[head, low:high, lanes] = jnp.take_along_axis(source, index, axis=1)
                 if low:
                     after = table[head : head + 1, 2 * REACH : 2 * REACH + 1]
                     bias_scr[head, 0:low, lanes] = jnp.broadcast_to(after, (low, LANES))
@@ -119,11 +124,13 @@
         low = (rest - middle.astype(F32)).astype(BF16)
         for part, piece in enumerate((high, middle, low)):
             embed_scr[part * padded : part * padded + classes, :] = piece
-        for tile in range(owned):
-            left_scr[tile * width : (tile + 1) * width, :] = left_ref[...]
+        left_scr[...] = jnp.zeros_like(left_scr)
+        for tile in range(LANES // width):
+            left_scr[tile, tile * width : (tile + 1) * width, :] = left_ref[...]
+        target_row = lax.broadcasted_iota(jnp.int32, gather_scr.shape, 0)
         gather_scr[...] = (
-            lax.broadcasted_iota(jnp.int32, gather_scr.shape, 0)
-            == lax.broadcasted_iota(jnp.int32, gather_scr.shape, 1) // owned
+            target_row % owners * owned + target_row // owners
+            == lax.broadcasted_iota(jnp.int32, gather_scr.shape, 1)
         ).astype(F32).astype(BF16)
         place = lax.broadcasted_iota(jnp.int32, (1, LANES), 1) // head_size
         for member in range(packed):
@@ -136,10 +143,6 @@
     place = lax.broadcasted_iota(jnp.int32, (1, LANES), 1) // head_size
     blank = jnp.zeros((), BF16)
     members = range(together)
-    diagonal = (
-        lax.broadcasted_iota(jnp.int32, (residues, owned * width), 0) % owned
-        == lax.broadcasted_iota(jnp.int32, (residues, owned * width), 1) // width
-    )
     rows = [step * together + k for k in members]
     initial, normed, query, keys, values, gates = [], [], [], [], [], []
     classes_iota = lax.broadcasted_iota(jnp.int32, (padded, residues), 0)
@@ -178,20 +181,25 @@
         updated = initial[k] + dot(whole, output_ref[...], ((1,), (0,)))
         updated_ref[k] = updated
         normed_two = normalize(updated, gain_two_ref[...])
-        narrow = normed_two.astype(BF16)
-        spread_left = dot(narrow, left_scr[...], ((1,), (1,)))
-        spread_left = jnp.where(diagonal, spread_left, 0.0).astype(BF16)
-        folded = dot(gather_scr[...], spread_left, ((1,), (0,)))
-        for tile in range(owned * width // LANES):
-            lanes = slice(tile * LANES, (tile + 1) * LANES)
-            owner_scr[tile, pl.ds(rows[k], owners, stride=count), :] = folded[:, lanes]
-        right = dot(right_ref[...], narrow, ((1,), (1,)))
-        for tile in range(residues // LANES):
-            lanes = slice(tile * LANES, (tile + 1) * LANES)
-            factor_scr[tile, pl.ds(rows[k], width, stride=count), :] = right[:, lanes]
+        narrow_scr[rows[k]] = normed_two.astype(BF16)
 
     @pl.when(step == pl.num_programs(0) - 1)
     def finish():
+        for k in range(count):
+            narrow = narrow_scr[k]
+            sorted_rows = dot(gather_scr[...], narrow, ((1,), (0,))).astype(BF16)
+            sorted_scr[:, k] = sorted_rows.reshape(owned, owners, features)
+            right = dot(right_ref[...], narrow, ((1,), (1,)))
+            for tile in range(residues // LANES):
+                lanes = slice(tile * LANES, (tile + 1) * LANES)
+                factor_scr[tile, pl.ds(k, width, stride=count), :] = right[:, lanes]
+        fold = LANES // width
+        for tile in range(owned // fold):
+            total = jnp.zeros((count * owners, LANES), F32)
+            for place in range(fold):
+                one = sorted_scr[tile * fold + place].reshape(count * owners, features)
+                total += dot(one, left_scr[place], ((1,), (1,)))
+            owner_scr[tile] = total
         right = jnp.concatenate([factor_scr[t] for t in range(residues // LANES)], axis=1)
         right = right.astype(BF16).reshape(width, count, residues)
         mine = lax.axis_index("wide") // inner
@@ -200,9 +208,10 @@
             target = meet(mine, shift, outer) * inner
             message_ref[0:width] = right
             for k in range(inner):
-                start = pl.multiple_of((target + k) * count, count)
                 for slab in range(slabs):
-                    block = [owner_scr[slab * per + t, pl.ds(start, count), :] for t in range(per)]
+                    block = [
+                        owner_scr[slab * per + t, pl.ds(target + k, count, stride=owners), :] for t in range(per)
+                    ]
                     message_ref[width + k * slabs + slab] = jnp.concatenate(block, axis=1).astype(BF16)
 
 
@@ -227,12 +236,14 @@
         ((heads, residues, residues), F32),
         ((heads, LANES), F32),
         ((3 * padded, features), BF16),
-        ((owned * width, features), BF16),
+        ((LANES // width, LANES, features), BF16),
         ((together, residues, packed * residues), BF16),
         ((together, packed * residues, 2 * LANES), BF16),
         ((residues // LANES, width * count, LANES), F32),
         ((owned * width // LANES, owners * count, LANES), F32),
-        ((owners, residues), BF16),
+        ((residues, residues), BF16),
+        ((count, residues, features), BF16),
+        ((owned, count, owners, features), BF16),
     ]
     return pl.pallas_call(
         functools.partial(attention_kernel, heads, owners, outer, together),

time: 56.2 us -> 54.5 us (0.970)
  Pallas kernels: 23.7 us -> 22 us
    pallas_call x1, Pallas kernels: 17.1 us -> 15.3 us  [attention(): pl.pallas_call(functools.partial(attention_kernel, heads, owners, outer,...]
where the time goes in v1:
time: 54.5 us; the launch traced here: 54.3 us
  Pallas kernels  22 us (40%)
  waiting for transfers between devices  19.1 us (35%)
  starting transfers between devices  11.6 us (21%)
  local copies, waits for them, and re-layouts  0.92 us (2%)
  between operations  0.73 us (1%)
    ppermute x15, waiting for transfers between devices, move(): return lax.ppermute(piece, 'wide', [(d, target(d)) for d in range(devices)])  19.1 us
    pallas_call x1, Pallas kernels, attention(): pl.pallas_call(functools.partial(attention_kernel, heads, owners, outer,...  15.3 us
    ppermute x15, starting transfers between devices, move(): return lax.ppermute(piece, 'wide', [(d, target(d)) for d in range(devices)])  11.6 us
    pallas_call x1, Pallas kernels, pair_features(): pl.pallas_call(functools.partial(pair_kernel, count, halves, inner), grid...  5.6 us
  transfers between devices with their start and end apart: 15, of which 5 were waited for; matrix products, arithmetic and copies ran while one was open for 0% of the time, Pallas kernels for 2%

profile of v1, /device:TPU:0, one launch (start us, length us, event | category | flops | bytes accessed | tf_op | source)
XLA Modules:
  0.0 54.3 jit_solution(15937954121335236793)
XLA Ops:
  0.7 15.3 %attention.1 = (f32[8,256,256]{2,1,0:T(8,128)}, bf16[40,8,256]{2,1,0:T(8,128)(2,1)}, bf16[40,8,256]{2,1,0:T(8,128)(2,1)}, bf16[40,8,256]{2,1,0:T(8,128)(2,1)}, bf16[40,8,256]{2,1,0:T(8,128)(2,1)}) custom-call(s32[8,256]{1,0:T(8,128)} %refs_0_.1, s32[1,256]{1,0:T(1,128)} %bitcast.12, f32[256,256]{1,0:T(8,128)} %refs_2_.1, f32[23,256]{1,0:T(8,128)} %refs_3_.1, ...), custom_call_target="tpu_custom_call" | custom-call | flops 5368709120 | bytes 2097152 | tf_op jit(solution)/shard_map/attention/pallas_call | solution.py:248
  16.0 3.1 %collective-permute-start = (bf16[40,8,256]{2,1,0:T(8,128)(2,1)}, bf16[40,8,256]{2,1,0:T(8,128)(2,1)S(1)}, u32[]{:S(2)}, u32[]{:S(2)}) collective-permute-start(bf16[40,8,256]{2,1,0:T(8,128)(2,1)} %get-tuple-element.13), channel_id=1, source_target_pairs={{0,4},{1,5},{2,6},{3,7},{4,0},{5,1},{6,2},{7,3},{8,12},{9,13},{10,... | collective-permute-start | bytes 491528 | tf_op jit(solution)/shard_map/ppermute | solution.py:271
  19.1 2.6 %collective-permute-start.1 = (bf16[40,8,256]{2,1,0:T(8,128)(2,1)}, bf16[40,8,256]{2,1,0:T(8,128)(2,1)S(1)}, u32[]{:S(2)}, u32[]{:S(2)}) collective-permute-start(bf16[40,8,256]{2,1,0:T(8,128)(2,1)} %get-tuple-element.14), channel_id=1, source_target_pairs={{0,8},{1,9},{2,10},{3,11},{4,12},{5,13},{6,14},{7,15},{8,0},{9,1},... | collective-permute-start | bytes 491528 | tf_op jit(solution)/shard_map/ppermute | solution.py:271
  21.7 0.0 collective-permute-start.2
  21.7 0.0 collective-permute-start.7
  21.7 1.7 %collective-permute-start.3 = (bf16[40,8,256]{2,1,0:T(8,128)(2,1)}, bf16[40,8,256]{2,1,0:T(8,128)(2,1)S(1)}, u32[]{:S(2)}, u32[]{:S(2)}) collective-permute-start(bf16[40,8,256]{2,1,0:T(8,128)(2,1)} %get-tuple-element.10.own_ref), channel_id=1, source_target_pairs={{0,2},{1,3},{2,0},{3,1},{4,6},{5,7},{6,4},{7,5},{8,10},{9,11},{10,... | collective-permute-start | bytes 491528 | tf_op jit(solution)/shard_map/ppermute | solution.py:271
  23.4 2.6 %collective-permute-done.rest_refs_1_ = bf16[40,8,256]{2,1,0:T(8,128)(2,1)S(1)} collective-permute-done((bf16[40,8,256]{2,1,0:T(8,128)(2,1)}, bf16[40,8,256]{2,1,0:T(8,128)(2,1)S(1)}, u32[]{:S(2)}, u32[]{:S(2)}) %collective-permute-start) | collective-permute-done | bytes 163872 | tf_op jit(solution)/shard_map/ppermute | solution.py:271
  26.0 0.0 collective-permute-start.8
  26.0 8.3 %collective-permute-done.1.rest_refs_2_ = bf16[40,8,256]{2,1,0:T(8,128)(2,1)S(1)} collective-permute-done((bf16[40,8,256]{2,1,0:T(8,128)(2,1)}, bf16[40,8,256]{2,1,0:T(8,128)(2,1)S(1)}, u32[]{:S(2)}, u32[]{:S(2)}) %collective-permute-start.1) | collective-permute-done | bytes 163872 | tf_op jit(solution)/shard_map/ppermute | solution.py:271
  34.3 1.5 %collective-permute-start.4 = (bf16[40,8,256]{2,1,0:T(8,128)(2,1)S(1)}, bf16[40,8,256]{2,1,0:T(8,128)(2,1)S(1)}, u32[]{:S(2)}, u32[]{:S(2)}) collective-permute-start(bf16[40,8,256]{2,1,0:T(8,128)(2,1)S(1)} %collective-permute-done.rest_refs_1_), channel_id=1, source_target_pairs={{0,2},{1,3},{2,0},{3,1},{4,6},{5,7},{6,4},{7,5},{8,10},{9,11},{10,... | collective-permute-start | bytes 491528 | tf_op jit(solution)/shard_map/ppermute | solution.py:271
  35.8 0.0 collective-permute-done.2.rest_refs_3_
  35.8 0.6 %collective-permute-start.5 = (bf16[40,8,256]{2,1,0:T(8,128)(2,1)S(1)}, bf16[40,8,256]{2,1,0:T(8,128)(2,1)S(1)}, u32[]{:S(2)}, u32[]{:S(2)}) collective-permute-start(bf16[40,8,256]{2,1,0:T(8,128)(2,1)S(1)} %collective-permute-done.1.rest_refs_2_), channel_id=1, source_target_pairs={{0,2},{1,3},{2,0},{3,1},{4,6},{5,7},{6,4},{7,5},{8,10},{9,11},{10,... | collective-permute-start | bytes 491528 | tf_op jit(solution)/shard_map/ppermute | solution.py:271
  36.4 1.5 %collective-permute-start.6 = (bf16[40,8,256]{2,1,0:T(8,128)(2,1)S(1)}, bf16[40,8,256]{2,1,0:T(8,128)(2,1)S(1)}, u32[]{:S(2)}, u32[]{:S(2)}) collective-permute-start(bf16[40,8,256]{2,1,0:T(8,128)(2,1)S(1)} %collective-permute-done.2.rest_refs_3_), channel_id=1, source_target_pairs={{0,2},{1,3},{2,0},{3,1},{4,6},{5,7},{6,4},{7,5},{8,10},{9,11},{10,... | collective-permute-start | bytes 491528 | tf_op jit(solution)/shard_map/ppermute | solution.py:271
  37.9 2.4 %collective-permute-done.4.rest_refs_5_ = bf16[40,8,256]{2,1,0:T(8,128)(2,1)S(1)} collective-permute-done((bf16[40,8,256]{2,1,0:T(8,128)(2,1)S(1)}, bf16[40,8,256]{2,1,0:T(8,128)(2,1)S(1)}, u32[]{:S(2)}, u32[]{:S(2)}) %collective-permute-start.4) | collective-permute-done | bytes 163872 | tf_op jit(solution)/shard_map/ppermute | solution.py:271
  40.4 0.0 collective-permute-start.11
  40.4 0.0 collective-permute-done.9.rest_refs_10_
  40.4 0.5 collective-permute-start.12
  40.9 3.0 %collective-permute-done.5.rest_refs_6_ = bf16[40,8,256]{2,1,0:T(8,128)(2,1)S(1)} collective-permute-done((bf16[40,8,256]{2,1,0:T(8,128)(2,1)S(1)}, bf16[40,8,256]{2,1,0:T(8,128)(2,1)S(1)}, u32[]{:S(2)}, u32[]{:S(2)}) %collective-permute-start.5) | collective-permute-done | bytes 163872 | tf_op jit(solution)/shard_map/ppermute | solution.py:271
  43.9 2.8 %collective-permute-done.6.rest_refs_7_ = bf16[40,8,256]{2,1,0:T(8,128)(2,1)S(1)} collective-permute-done((bf16[40,8,256]{2,1,0:T(8,128)(2,1)S(1)}, bf16[40,8,256]{2,1,0:T(8,128)(2,1)S(1)}, u32[]{:S(2)}, u32[]{:S(2)}) %collective-permute-start.6) | collective-permute-done | bytes 163872 | tf_op jit(solution)/shard_map/ppermute | solution.py:271
  46.7 0.0 collective-permute-start.14
  46.7 0.9 %copy-done.1 = bf16[40,8,256]{2,1,0:T(8,128)(2,1)S(1)} copy-done((bf16[40,8,256]{2,1,0:T(8,128)(2,1)S(1)}, bf16[40,8,256]{2,1,0:T(8,128)(2,1)}, u32[]{:S(2)}) %copy-start.1) | copy-done | bytes 163864
  47.6 1.1 %order.1 = (bf16[128,1024]{1,0:T(8,128)(2,1)S(1)}, bf16[40,8,256]{2,1,0:T(8,128)(2,1)S(1)}) custom-call(bf16[1024,128]{1,0:T(8,128)(2,1)S(1)} %copy-done, bf16[40,8,256]{2,1,0:T(8,128)(2,1)S(1)} %copy-done.1), custom_call_target="tpu_custom_call" | custom-call | bytes 524288 | tf_op jit(solution)/shard_map/order/pallas_call | solution.py:299
  48.7 0.0 collective-permute-done.11.rest_refs_12_
  48.7 5.6 %pair.1 = f32[16,256,128]{2,1,0:T(8,128)} custom-call(bf16[128,1024]{1,0:T(8,128)(2,1)S(1)} %get-tuple-element.11.weight_ref, f32[1,128]{1,0:T(1,128)S(1)} %bitcast.8, bf16[40,8,256]{2,1,0:T(8,128)(2,1)S(1)} %get-tuple-element.12.rest_refs_0_, bf16[40,8,256]{2,1,0:T(8,128)(2,1)S(1)} %collective-permute-done.rest_refs_1_, ...), custom_call_target="tpu_custom_call" | custom-call | tf_op jit(solution)/shard_map/pair/pallas_call | solution.py:383
  (15 shorter events, 0.0 us)
Async XLA Ops:
  0.6 46.0 %copy-start = (bf16[1024,128]{1,0:T(8,128)(2,1)S(1)}, bf16[1024,128]{1,0:T(8,128)(2,1)}, u32[]{:S(2)}) copy-start(bf16[1024,128]{1,0:T(8,128)(2,1)} %weight_ref.1) | copy-start | bytes 786436
  0.6 48.1 %copy-start.2 = (f32[128]{0:T(128)S(1)}, f32[128]{0:T(128)}, u32[]{:S(2)}) copy-start(f32[128]{0:T(128)} %param.33) | copy-start | bytes 1540
  16.0 10.0 %collective-permute-start = (bf16[40,8,256]{2,1,0:T(8,128)(2,1)}, bf16[40,8,256]{2,1,0:T(8,128)(2,1)S(1)}, u32[]{:S(2)}, u32[]{:S(2)}) collective-permute-start(bf16[40,8,256]{2,1,0:T(8,128)(2,1)} %get-tuple-element.13), channel_id=1, source_target_pairs={{0,4},{1,5},{2,6},{3,7},{4,0},{5,1},{6,2},{7,3},{8,12},{9,13},{10,... | collective-permute-start | bytes 491528 | tf_op jit(solution)/shard_map/ppermute | solution.py:271
  19.1 15.2 %collective-permute-start.1 = (bf16[40,8,256]{2,1,0:T(8,128)(2,1)}, bf16[40,8,256]{2,1,0:T(8,128)(2,1)S(1)}, u32[]{:S(2)}, u32[]{:S(2)}) collective-permute-start(bf16[40,8,256]{2,1,0:T(8,128)(2,1)} %get-tuple-element.14), channel_id=1, source_target_pairs={{0,8},{1,9},{2,10},{3,11},{4,12},{5,13},{6,14},{7,15},{8,0},{9,1},... | collective-permute-start | bytes 491528 | tf_op jit(solution)/shard_map/ppermute | solution.py:271
  21.7 14.1 %collective-permute-start.2 = (bf16[40,8,256]{2,1,0:T(8,128)(2,1)}, bf16[40,8,256]{2,1,0:T(8,128)(2,1)S(1)}, u32[]{:S(2)}, u32[]{:S(2)}) collective-permute-start(bf16[40,8,256]{2,1,0:T(8,128)(2,1)} %get-tuple-element.15), channel_id=1, source_target_pairs={{0,12},{1,13},{2,14},{3,15},{4,8},{5,9},{6,10},{7,11},{8,4},{9,5},... | collective-permute-start | bytes 491528 | tf_op jit(solution)/shard_map/ppermute | solution.py:271
  21.7 14.1 %collective-permute-start.7 = (bf16[40,8,256]{2,1,0:T(8,128)(2,1)}, bf16[40,8,256]{2,1,0:T(8,128)(2,1)S(1)}, u32[]{:S(2)}, u32[]{:S(2)}) collective-permute-start(bf16[40,8,256]{2,1,0:T(8,128)(2,1)} %get-tuple-element.10.own_ref), channel_id=1, source_target_pairs={{0,1},{1,0},{2,3},{3,2},{4,5},{5,4},{6,7},{7,6},{8,9},{9,8},{10,11... | collective-permute-start | bytes 491528 | tf_op jit(solution)/shard_map/ppermute | solution.py:271
  21.7 14.7 %collective-permute-start.3 = (bf16[40,8,256]{2,1,0:T(8,128)(2,1)}, bf16[40,8,256]{2,1,0:T(8,128)(2,1)S(1)}, u32[]{:S(2)}, u32[]{:S(2)}) collective-permute-start(bf16[40,8,256]{2,1,0:T(8,128)(2,1)} %get-tuple-element.10.own_ref), channel_id=1, source_target_pairs={{0,2},{1,3},{2,0},{3,1},{4,6},{5,7},{6,4},{7,5},{8,10},{9,11},{10,... | collective-permute-start | bytes 491528 | tf_op jit(solution)/shard_map/ppermute | solution.py:271
  26.0 11.9 %collective-permute-start.8 = (bf16[40,8,256]{2,1,0:T(8,128)(2,1)S(1)}, bf16[40,8,256]{2,1,0:T(8,128)(2,1)S(1)}, u32[]{:S(2)}, u32[]{:S(2)}) collective-permute-start(bf16[40,8,256]{2,1,0:T(8,128)(2,1)S(1)} %collective-permute-done.rest_refs_1_), channel_id=1, source_target_pairs={{0,1},{1,0},{2,3},{3,2},{4,5},{5,4},{6,7},{7,6},{8,9},{9,8},{10,11... | collective-permute-start | bytes 491528 | tf_op jit(solution)/shard_map/ppermute | solution.py:271
  34.3 6.1 %collective-permute-start.4 = (bf16[40,8,256]{2,1,0:T(8,128)(2,1)S(1)}, bf16[40,8,256]{2,1,0:T(8,128)(2,1)S(1)}, u32[]{:S(2)}, u32[]{:S(2)}) collective-permute-start(bf16[40,8,256]{2,1,0:T(8,128)(2,1)S(1)} %collective-permute-done.rest_refs_1_), channel_id=1, source_target_pairs={{0,2},{1,3},{2,0},{3,1},{4,6},{5,7},{6,4},{7,5},{8,10},{9,11},{10,... | collective-permute-start | bytes 491528 | tf_op jit(solution)/shard_map/ppermute | solution.py:271
  35.8 4.5 %collective-permute-start.9 = (bf16[40,8,256]{2,1,0:T(8,128)(2,1)S(1)}, bf16[40,8,256]{2,1,0:T(8,128)(2,1)S(1)}, u32[]{:S(2)}, u32[]{:S(2)}) collective-permute-start(bf16[40,8,256]{2,1,0:T(8,128)(2,1)S(1)} %collective-permute-done.1.rest_refs_2_), channel_id=1, source_target_pairs={{0,1},{1,0},{2,3},{3,2},{4,5},{5,4},{6,7},{7,6},{8,9},{9,8},{10,11... | collective-permute-start | bytes 491528 | tf_op jit(solution)/shard_map/ppermute | solution.py:271
  35.8 8.0 %collective-permute-start.5 = (bf16[40,8,256]{2,1,0:T(8,128)(2,1)S(1)}, bf16[40,8,256]{2,1,0:T(8,128)(2,1)S(1)}, u32[]{:S(2)}, u32[]{:S(2)}) collective-permute-start(bf16[40,8,256]{2,1,0:T(8,128)(2,1)S(1)} %collective-permute-done.1.rest_refs_2_), channel_id=1, source_target_pairs={{0,2},{1,3},{2,0},{3,1},{4,6},{5,7},{6,4},{7,5},{8,10},{9,11},{10,... | collective-permute-start | bytes 491528 | tf_op jit(solution)/shard_map/ppermute | solution.py:271
  36.4 10.2 %collective-permute-start.6 = (bf16[40,8,256]{2,1,0:T(8,128)(2,1)S(1)}, bf16[40,8,256]{2,1,0:T(8,128)(2,1)S(1)}, u32[]{:S(2)}, u32[]{:S(2)}) collective-permute-start(bf16[40,8,256]{2,1,0:T(8,128)(2,1)S(1)} %collective-permute-done.2.rest_refs_3_), channel_id=1, source_target_pairs={{0,2},{1,3},{2,0},{3,1},{4,6},{5,7},{6,4},{7,5},{8,10},{9,11},{10,... | collective-permute-start | bytes 491528 | tf_op jit(solution)/shard_map/ppermute | solution.py:271
  37.9 10.7 %collective-permute-start.10 = (bf16[40,8,256]{2,1,0:T(8,128)(2,1)S(1)}, bf16[40,8,256]{2,1,0:T(8,128)(2,1)S(1)}, u32[]{:S(2)}, u32[]{:S(2)}) collective-permute-start(bf16[40,8,256]{2,1,0:T(8,128)(2,1)S(1)} %collective-permute-done.2.rest_refs_3_), channel_id=1, source_target_pairs={{0,1},{1,0},{2,3},{3,2},{4,5},{5,4},{6,7},{7,6},{8,9},{9,8},{10,11... | collective-permute-start | bytes 491528 | tf_op jit(solution)/shard_map/ppermute | solution.py:271
  40.4 8.3 %collective-permute-start.11 = (bf16[40,8,256]{2,1,0:T(8,128)(2,1)S(1)}, bf16[40,8,256]{2,1,0:T(8,128)(2,1)S(1)}, u32[]{:S(2)}, u32[]{:S(2)}) collective-permute-start(bf16[40,8,256]{2,1,0:T(8,128)(2,1)S(1)} %collective-permute-done.3.rest_refs_4_), channel_id=1, source_target_pairs={{0,1},{1,0},{2,3},{3,2},{4,5},{5,4},{6,7},{7,6},{8,9},{9,8},{10,11... | collective-permute-start | bytes 491528 | tf_op jit(solution)/shard_map/ppermute | solution.py:271
  40.4 8.3 %collective-permute-start.12 = (bf16[40,8,256]{2,1,0:T(8,128)(2,1)S(1)}, bf16[40,8,256]{2,1,0:T(8,128)(2,1)S(1)}, u32[]{:S(2)}, u32[]{:S(2)}) collective-permute-start(bf16[40,8,256]{2,1,0:T(8,128)(2,1)S(1)} %collective-permute-done.4.rest_refs_5_), channel_id=1, source_target_pairs={{0,1},{1,0},{2,3},{3,2},{4,5},{5,4},{6,7},{7,6},{8,9},{9,8},{10,11... | collective-permute-start | bytes 491528 | tf_op jit(solution)/shard_map/ppermute | solution.py:271
  43.9 4.8 %collective-permute-start.13 = (bf16[40,8,256]{2,1,0:T(8,128)(2,1)S(1)}, bf16[40,8,256]{2,1,0:T(8,128)(2,1)S(1)}, u32[]{:S(2)}, u32[]{:S(2)}) collective-permute-start(bf16[40,8,256]{2,1,0:T(8,128)(2,1)S(1)} %collective-permute-done.5.rest_refs_6_), channel_id=1, source_target_pairs={{0,1},{1,0},{2,3},{3,2},{4,5},{5,4},{6,7},{7,6},{8,9},{9,8},{10,11... | collective-permute-start | bytes 491528 | tf_op jit(solution)/shard_map/ppermute | solution.py:271
  46.7 2.0 %collective-permute-start.14 = (bf16[40,8,256]{2,1,0:T(8,128)(2,1)S(1)}, bf16[40,8,256]{2,1,0:T(8,128)(2,1)S(1)}, u32[]{:S(2)}, u32[]{:S(2)}) collective-permute-start(bf16[40,8,256]{2,1,0:T(8,128)(2,1)S(1)} %collective-permute-done.6.rest_refs_7_), channel_id=1, source_target_pairs={{0,1},{1,0},{2,3},{3,2},{4,5},{5,4},{6,7},{7,6},{8,9},{9,8},{10,11... | collective-permute-start | bytes 491528 | tf_op jit(solution)/shard_map/ppermute | solution.py:271
  46.7 0.9 %copy-start.1 = (bf16[40,8,256]{2,1,0:T(8,128)(2,1)S(1)}, bf16[40,8,256]{2,1,0:T(8,128)(2,1)}, u32[]{:S(2)}) copy-start(bf16[40,8,256]{2,1,0:T(8,128)(2,1)} %get-tuple-element.10.own_ref) | copy-start | bytes 491524

commit v2 on v1

--- a/solution.py
+++ b/solution.py
@@ -11,6 +11,7 @@
 
 REACH = 32
 LANES = 128
+ROWS = 1024
 F32 = jnp.float32
 BF16 = jnp.bfloat16
 
@@ -144,20 +145,23 @@
     blank = jnp.zeros((), BF16)
     members = range(together)
     rows = [step * together + k for k in members]
-    initial, normed, query, keys, values, gates = [], [], [], [], [], []
+    initial, query, keys, values, gates = [], [], [], [], []
     classes_iota = lax.broadcasted_iota(jnp.int32, (padded, residues), 0)
     for k in members:
         tokens = tokens_ref[pl.ds(rows[k], 1), :]
         onehot = (classes_iota == tokens).astype(F32).astype(BF16)
         onehot = jnp.concatenate([onehot, onehot, onehot], axis=0)
         initial.append(dot(onehot, embed_scr[...], ((0,), (0,))) + target_ref[...])
-    for k in members:
-        normed.append(normalize(initial[k], gain_ref[...]).astype(BF16))
-    for k in members:
-        product = dot(normed[k], query_ref[...], ((1,), (0,)))
-        query.append((product * (1.0 / head_size**0.5)).astype(BF16))
-        keys.append(dot(normed[k], key_ref[...], ((1,), (0,))).astype(BF16))
-        values.append(dot(normed[k], value_ref[...], ((1,), (0,))).astype(BF16))
+    both_initial = jnp.concatenate(initial, axis=0)
+    both_normed = normalize(both_initial, gain_ref[...]).astype(BF16)
+    spans = [slice(k * residues, (k + 1) * residues) for k in members]
+    product = dot(both_normed, query_ref[...], ((1,), (0,)))
+    product = (product * (1.0 / head_size**0.5)).astype(BF16)
+    query = [product[span] for span in spans]
+    product = dot(both_normed, key_ref[...], ((1,), (0,))).astype(BF16)
+    keys = [product[span] for span in spans]
+    product = dot(both_normed, value_ref[...], ((1,), (0,))).astype(BF16)
+    values = [product[span] for span in spans]
     mixed = [[] for _ in members]
     for group in range(groups):
         lanes = slice(group * LANES, (group + 1) * LANES)
@@ -174,14 +178,14 @@
         for k in members:
             both = dot(weights_scr[k], mixer_scr[k], ((1,), (0,)))
             mixed[k].append(both[:, :LANES] / both[:, LANES:])
+    gates = jax.nn.sigmoid(dot(both_normed, gate_ref[...], ((1,), (0,))) + gate_bias_ref[...])
+    whole = jnp.concatenate([jnp.concatenate(mixed[k], axis=1) for k in members], axis=0)
+    whole = (whole * gates).astype(BF16)
+    updated = both_initial + dot(whole, output_ref[...], ((1,), (0,)))
+    normed_two = normalize(updated, gain_two_ref[...]).astype(BF16)
     for k in members:
-        gates.append(jax.nn.sigmoid(dot(normed[k], gate_ref[...], ((1,), (0,))) + gate_bias_ref[...]))
-    for k in members:
-        whole = (jnp.concatenate(mixed[k], axis=1) * gates[k]).astype(BF16)
-        updated = initial[k] + dot(whole, output_ref[...], ((1,), (0,)))
-        updated_ref[k] = updated
-        normed_two = normalize(updated, gain_two_ref[...])
-        narrow_scr[rows[k]] = normed_two.astype(BF16)
+        updated_ref[k] = updated[spans[k]]
+        narrow_scr[rows[k]] = normed_two[spans[k]]
 
     @pl.when(step == pl.num_programs(0) - 1)
     def finish():
@@ -225,7 +229,7 @@
     width = right_weight.shape[0]
     owned = residues // owners
     padded = -(-embed.shape[0] // 32) * 32
-    together = 2 if count % 2 == 0 else 1
+    together = math.gcd(count, max(1, ROWS // residues))
     whole = lambda x: pl.BlockSpec(x.shape, lambda s, n=x.ndim: (0,) * n)
     slabs = owned * width // residues
     message = (width + owners // outer * slabs, count, residues)

time: 54.5 us -> 53.4 us (0.980)
  Pallas kernels: 22 us -> 20.9 us
    pallas_call x1, Pallas kernels: 15.3 us -> 14.2 us  [attention(): pl.pallas_call(functools.partial(attention_kernel, heads, owners, outer,...]
where the time goes in v2:
time: 53.4 us; the launch traced here: 53.2 us
  Pallas kernels  20.9 us (39%)
  waiting for transfers between devices  19.1 us (36%)
  starting transfers between devices  11.6 us (22%)
  local copies, waits for them, and re-layouts  0.92 us (2%)
  between operations  0.73 us (1%)
    ppermute x15, waiting for transfers between devices, move(): return lax.ppermute(piece, 'wide', [(d, target(d)) for d in range(devices)])  19.1 us
    pallas_call x1, Pallas kernels, attention(): pl.pallas_call(functools.partial(attention_kernel, heads, owners, outer,...  14.2 us
    ppermute x15, starting transfers between devices, move(): return lax.ppermute(piece, 'wide', [(d, target(d)) for d in range(devices)])  11.6 us
    pallas_call x1, Pallas kernels, pair_features(): pl.pallas_call(functools.partial(pair_kernel, count, halves, inner), grid...  5.59 us
    pallas_call x1, Pallas kernels, ordered(): pl.pallas_call(order_kernel, in_specs=[pl.BlockSpec(weight.shape, lambda:...  1.07 us
  transfers between devices with their start and end apart: 15, of which 5 were waited for; matrix products, arithmetic and copies ran while one was open for 0% of the time, Pallas kernels for 2%

profile of v2, /device:TPU:0, one launch (start us, length us, event | category | flops | bytes accessed | tf_op | source)
XLA Modules:
  0.0 53.2 jit_solution(4043048826777058149)
XLA Ops:
  0.7 14.2 %attention.1 = (f32[8,256,256]{2,1,0:T(8,128)}, bf16[40,8,256]{2,1,0:T(8,128)(2,1)}, bf16[40,8,256]{2,1,0:T(8,128)(2,1)}, bf16[40,8,256]{2,1,0:T(8,128)(2,1)}, bf16[40,8,256]{2,1,0:T(8,128)(2,1)}) custom-call(s32[8,256]{1,0:T(8,128)} %refs_0_.1, s32[1,256]{1,0:T(1,128)} %bitcast.12, f32[256,256]{1,0:T(8,128)} %refs_2_.1, f32[23,256]{1,0:T(8,128)} %refs_3_.1, ...), custom_call_target="tpu_custom_call" | custom-call | flops 5368709120 | bytes 2097152 | tf_op jit(solution)/shard_map/attention/pallas_call | solution.py:252
  14.9 3.1 %collective-permute-start = (bf16[40,8,256]{2,1,0:T(8,128)(2,1)}, bf16[40,8,256]{2,1,0:T(8,128)(2,1)S(1)}, u32[]{:S(2)}, u32[]{:S(2)}) collective-permute-start(bf16[40,8,256]{2,1,0:T(8,128)(2,1)} %get-tuple-element.13), channel_id=1, source_target_pairs={{0,4},{1,5},{2,6},{3,7},{4,0},{5,1},{6,2},{7,3},{8,12},{9,13},{10,... | collective-permute-start | bytes 491528 | tf_op jit(solution)/shard_map/ppermute | solution.py:275
  18.0 2.6 %collective-permute-start.1 = (bf16[40,8,256]{2,1,0:T(8,128)(2,1)}, bf16[40,8,256]{2,1,0:T(8,128)(2,1)S(1)}, u32[]{:S(2)}, u32[]{:S(2)}) collective-permute-start(bf16[40,8,256]{2,1,0:T(8,128)(2,1)} %get-tuple-element.14), channel_id=1, source_target_pairs={{0,8},{1,9},{2,10},{3,11},{4,12},{5,13},{6,14},{7,15},{8,0},{9,1},... | collective-permute-start | bytes 491528 | tf_op jit(solution)/shard_map/ppermute | solution.py:275
  20.6 0.0 collective-permute-start.7
  20.6 1.7 %collective-permute-start.3 = (bf16[40,8,256]{2,1,0:T(8,128)(2,1)}, bf16[40,8,256]{2,1,0:T(8,128)(2,1)S(1)}, u32[]{:S(2)}, u32[]{:S(2)}) collective-permute-start(bf16[40,8,256]{2,1,0:T(8,128)(2,1)} %get-tuple-element.10.own_ref), channel_id=1, source_target_pairs={{0,2},{1,3},{2,0},{3,1},{4,6},{5,7},{6,4},{7,5},{8,10},{9,11},{10,... | collective-permute-start | bytes 491528 | tf_op jit(solution)/shard_map/ppermute | solution.py:275
  22.3 2.6 %collective-permute-done.rest_refs_1_ = bf16[40,8,256]{2,1,0:T(8,128)(2,1)S(1)} collective-permute-done((bf16[40,8,256]{2,1,0:T(8,128)(2,1)}, bf16[40,8,256]{2,1,0:T(8,128)(2,1)S(1)}, u32[]{:S(2)}, u32[]{:S(2)}) %collective-permute-start) | collective-permute-done | bytes 163872 | tf_op jit(solution)/shard_map/ppermute | solution.py:275
  24.9 0.0 collective-permute-start.8
  24.9 8.3 %collective-permute-done.1.rest_refs_2_ = bf16[40,8,256]{2,1,0:T(8,128)(2,1)S(1)} collective-permute-done((bf16[40,8,256]{2,1,0:T(8,128)(2,1)}, bf16[40,8,256]{2,1,0:T(8,128)(2,1)S(1)}, u32[]{:S(2)}, u32[]{:S(2)}) %collective-permute-start.1) | collective-permute-done | bytes 163872 | tf_op jit(solution)/shard_map/ppermute | solution.py:275
  33.2 1.5 %collective-permute-start.4 = (bf16[40,8,256]{2,1,0:T(8,128)(2,1)S(1)}, bf16[40,8,256]{2,1,0:T(8,128)(2,1)S(1)}, u32[]{:S(2)}, u32[]{:S(2)}) collective-permute-start(bf16[40,8,256]{2,1,0:T(8,128)(2,1)S(1)} %collective-permute-done.rest_refs_1_), channel_id=1, source_target_pairs={{0,2},{1,3},{2,0},{3,1},{4,6},{5,7},{6,4},{7,5},{8,10},{9,11},{10,... | collective-permute-start | bytes 491528 | tf_op jit(solution)/shard_map/ppermute | solution.py:275
  34.7 0.0 collective-permute-done.2.rest_refs_3_
  34.7 0.0 collective-permute-start.9
  34.7 0.0 collective-permute-done.7.rest_refs_8_
  34.7 0.6 %collective-permute-start.5 = (bf16[40,8,256]{2,1,0:T(8,128)(2,1)S(1)}, bf16[40,8,256]{2,1,0:T(8,128)(2,1)S(1)}, u32[]{:S(2)}, u32[]{:S(2)}) collective-permute-start(bf16[40,8,256]{2,1,0:T(8,128)(2,1)S(1)} %collective-permute-done.1.rest_refs_2_), channel_id=1, source_target_pairs={{0,2},{1,3},{2,0},{3,1},{4,6},{5,7},{6,4},{7,5},{8,10},{9,11},{10,... | collective-permute-start | bytes 491528 | tf_op jit(solution)/shard_map/ppermute | solution.py:275
  35.3 1.5 %collective-permute-start.6 = (bf16[40,8,256]{2,1,0:T(8,128)(2,1)S(1)}, bf16[40,8,256]{2,1,0:T(8,128)(2,1)S(1)}, u32[]{:S(2)}, u32[]{:S(2)}) collective-permute-start(bf16[40,8,256]{2,1,0:T(8,128)(2,1)S(1)} %collective-permute-done.2.rest_refs_3_), channel_id=1, source_target_pairs={{0,2},{1,3},{2,0},{3,1},{4,6},{5,7},{6,4},{7,5},{8,10},{9,11},{10,... | collective-permute-start | bytes 491528 | tf_op jit(solution)/shard_map/ppermute | solution.py:275
  36.8 0.0 collective-permute-done.8.rest_refs_9_
  36.8 2.4 %collective-permute-done.4.rest_refs_5_ = bf16[40,8,256]{2,1,0:T(8,128)(2,1)S(1)} collective-permute-done((bf16[40,8,256]{2,1,0:T(8,128)(2,1)S(1)}, bf16[40,8,256]{2,1,0:T(8,128)(2,1)S(1)}, u32[]{:S(2)}, u32[]{:S(2)}) %collective-permute-start.4) | collective-permute-done | bytes 163872 | tf_op jit(solution)/shard_map/ppermute | solution.py:275
  39.3 0.0 collective-permute-start.11
  39.3 0.0 collective-permute-done.9.rest_refs_10_
  39.3 0.5 collective-permute-start.12
  39.8 3.0 %collective-permute-done.5.rest_refs_6_ = bf16[40,8,256]{2,1,0:T(8,128)(2,1)S(1)} collective-permute-done((bf16[40,8,256]{2,1,0:T(8,128)(2,1)S(1)}, bf16[40,8,256]{2,1,0:T(8,128)(2,1)S(1)}, u32[]{:S(2)}, u32[]{:S(2)}) %collective-permute-start.5) | collective-permute-done | bytes 163872 | tf_op jit(solution)/shard_map/ppermute | solution.py:275
  42.8 2.8 %collective-permute-done.6.rest_refs_7_ = bf16[40,8,256]{2,1,0:T(8,128)(2,1)S(1)} collective-permute-done((bf16[40,8,256]{2,1,0:T(8,128)(2,1)S(1)}, bf16[40,8,256]{2,1,0:T(8,128)(2,1)S(1)}, u32[]{:S(2)}, u32[]{:S(2)}) %collective-permute-start.6) | collective-permute-done | bytes 163872 | tf_op jit(solution)/shard_map/ppermute | solution.py:275
  45.6 0.9 %copy-done.1 = bf16[40,8,256]{2,1,0:T(8,128)(2,1)S(1)} copy-done((bf16[40,8,256]{2,1,0:T(8,128)(2,1)S(1)}, bf16[40,8,256]{2,1,0:T(8,128)(2,1)}, u32[]{:S(2)}) %copy-start.1) | copy-done | bytes 163864
  46.5 1.1 %order.1 = (bf16[128,1024]{1,0:T(8,128)(2,1)S(1)}, bf16[40,8,256]{2,1,0:T(8,128)(2,1)S(1)}) custom-call(bf16[1024,128]{1,0:T(8,128)(2,1)S(1)} %copy-done, bf16[40,8,256]{2,1,0:T(8,128)(2,1)S(1)} %copy-done.1), custom_call_target="tpu_custom_call" | custom-call | bytes 524288 | tf_op jit(solution)/shard_map/order/pallas_call | solution.py:303
  47.6 5.6 %pair.1 = f32[16,256,128]{2,1,0:T(8,128)} custom-call(bf16[128,1024]{1,0:T(8,128)(2,1)S(1)} %get-tuple-element.11.weight_ref, f32[1,128]{1,0:T(1,128)S(1)} %bitcast.8, bf16[40,8,256]{2,1,0:T(8,128)(2,1)S(1)} %get-tuple-element.12.rest_refs_0_, bf16[40,8,256]{2,1,0:T(8,128)(2,1)S(1)} %collective-permute-done.rest_refs_1_, ...), custom_call_target="tpu_custom_call" | custom-call | tf_op jit(solution)/shard_map/pair/pallas_call | solution.py:387
  (15 shorter events, 0.0 us)
Async XLA Ops:
  0.6 44.9 %copy-start = (bf16[1024,128]{1,0:T(8,128)(2,1)S(1)}, bf16[1024,128]{1,0:T(8,128)(2,1)}, u32[]{:S(2)}) copy-start(bf16[1024,128]{1,0:T(8,128)(2,1)} %weight_ref.1) | copy-start | bytes 786436
  0.6 47.0 %copy-start.2 = (f32[128]{0:T(128)S(1)}, f32[128]{0:T(128)}, u32[]{:S(2)}) copy-start(f32[128]{0:T(128)} %param.33) | copy-start | bytes 1540
  14.9 10.0 %collective-permute-start = (bf16[40,8,256]{2,1,0:T(8,128)(2,1)}, bf16[40,8,256]{2,1,0:T(8,128)(2,1)S(1)}, u32[]{:S(2)}, u32[]{:S(2)}) collective-permute-start(bf16[40,8,256]{2,1,0:T(8,128)(2,1)} %get-tuple-element.13), channel_id=1, source_target_pairs={{0,4},{1,5},{2,6},{3,7},{4,0},{5,1},{6,2},{7,3},{8,12},{9,13},{10,... | collective-permute-start | bytes 491528 | tf_op jit(solution)/shard_map/ppermute | solution.py:275
  18.0 15.2 %collective-permute-start.1 = (bf16[40,8,256]{2,1,0:T(8,128)(2,1)}, bf16[40,8,256]{2,1,0:T(8,128)(2,1)S(1)}, u32[]{:S(2)}, u32[]{:S(2)}) collective-permute-start(bf16[40,8,256]{2,1,0:T(8,128)(2,1)} %get-tuple-element.14), channel_id=1, source_target_pairs={{0,8},{1,9},{2,10},{3,11},{4,12},{5,13},{6,14},{7,15},{8,0},{9,1},... | collective-permute-start | bytes 491528 | tf_op jit(solution)/shard_map/ppermute | solution.py:275
  20.6 14.1 %collective-permute-start.2 = (bf16[40,8,256]{2,1,0:T(8,128)(2,1)}, bf16[40,8,256]{2,1,0:T(8,128)(2,1)S(1)}, u32[]{:S(2)}, u32[]{:S(2)}) collective-permute-start(bf16[40,8,256]{2,1,0:T(8,128)(2,1)} %get-tuple-element.15), channel_id=1, source_target_pairs={{0,12},{1,13},{2,14},{3,15},{4,8},{5,9},{6,10},{7,11},{8,4},{9,5},... | collective-permute-start | bytes 491528 | tf_op jit(solution)/shard_map/ppermute | solution.py:275
  20.6 14.1 %collective-permute-start.7 = (bf16[40,8,256]{2,1,0:T(8,128)(2,1)}, bf16[40,8,256]{2,1,0:T(8,128)(2,1)S(1)}, u32[]{:S(2)}, u32[]{:S(2)}) collective-permute-start(bf16[40,8,256]{2,1,0:T(8,128)(2,1)} %get-tuple-element.10.own_ref), channel_id=1, source_target_pairs={{0,1},{1,0},{2,3},{3,2},{4,5},{5,4},{6,7},{7,6},{8,9},{9,8},{10,11... | collective-permute-start | bytes 491528 | tf_op jit(solution)/shard_map/ppermute | solution.py:275
  20.6 14.7 %collective-permute-start.3 = (bf16[40,8,256]{2,1,0:T(8,128)(2,1)}, bf16[40,8,256]{2,1,0:T(8,128)(2,1)S(1)}, u32[]{:S(2)}, u32[]{:S(2)}) collective-permute-start(bf16[40,8,256]{2,1,0:T(8,128)(2,1)} %get-tuple-element.10.own_ref), channel_id=1, source_target_pairs={{0,2},{1,3},{2,0},{3,1},{4,6},{5,7},{6,4},{7,5},{8,10},{9,11},{10,... | collective-permute-start | bytes 491528 | tf_op jit(solution)/shard_map/ppermute | solution.py:275
  24.9 11.9 %collective-permute-start.8 = (bf16[40,8,256]{2,1,0:T(8,128)(2,1)S(1)}, bf16[40,8,256]{2,1,0:T(8,128)(2,1)S(1)}, u32[]{:S(2)}, u32[]{:S(2)}) collective-permute-start(bf16[40,8,256]{2,1,0:T(8,128)(2,1)S(1)} %collective-permute-done.rest_refs_1_), channel_id=1, source_target_pairs={{0,1},{1,0},{2,3},{3,2},{4,5},{5,4},{6,7},{7,6},{8,9},{9,8},{10,11... | collective-permute-start | bytes 491528 | tf_op jit(solution)/shard_map/ppermute | solution.py:275
  33.2 6.1 %collective-permute-start.4 = (bf16[40,8,256]{2,1,0:T(8,128)(2,1)S(1)}, bf16[40,8,256]{2,1,0:T(8,128)(2,1)S(1)}, u32[]{:S(2)}, u32[]{:S(2)}) collective-permute-start(bf16[40,8,256]{2,1,0:T(8,128)(2,1)S(1)} %collective-permute-done.rest_refs_1_), channel_id=1, source_target_pairs={{0,2},{1,3},{2,0},{3,1},{4,6},{5,7},{6,4},{7,5},{8,10},{9,11},{10,... | collective-permute-start | bytes 491528 | tf_op jit(solution)/shard_map/ppermute | solution.py:275
  34.7 4.5 %collective-permute-start.9 = (bf16[40,8,256]{2,1,0:T(8,128)(2,1)S(1)}, bf16[40,8,256]{2,1,0:T(8,128)(2,1)S(1)}, u32[]{:S(2)}, u32[]{:S(2)}) collective-permute-start(bf16[40,8,256]{2,1,0:T(8,128)(2,1)S(1)} %collective-permute-done.1.rest_refs_2_), channel_id=1, source_target_pairs={{0,1},{1,0},{2,3},{3,2},{4,5},{5,4},{6,7},{7,6},{8,9},{9,8},{10,11... | collective-permute-start | bytes 491528 | tf_op jit(solution)/shard_map/ppermute | solution.py:275
  34.7 8.0 %collective-permute-start.5 = (bf16[40,8,256]{2,1,0:T(8,128)(2,1)S(1)}, bf16[40,8,256]{2,1,0:T(8,128)(2,1)S(1)}, u32[]{:S(2)}, u32[]{:S(2)}) collective-permute-start(bf16[40,8,256]{2,1,0:T(8,128)(2,1)S(1)} %collective-permute-done.1.rest_refs_2_), channel_id=1, source_target_pairs={{0,2},{1,3},{2,0},{3,1},{4,6},{5,7},{6,4},{7,5},{8,10},{9,11},{10,... | collective-permute-start | bytes 491528 | tf_op jit(solution)/shard_map/ppermute | solution.py:275
  35.3 10.2 %collective-permute-start.6 = (bf16[40,8,256]{2,1,0:T(8,128)(2,1)S(1)}, bf16[40,8,256]{2,1,0:T(8,128)(2,1)S(1)}, u32[]{:S(2)}, u32[]{:S(2)}) collective-permute-start(bf16[40,8,256]{2,1,0:T(8,128)(2,1)S(1)} %collective-permute-done.2.rest_refs_3_), channel_id=1, source_target_pairs={{0,2},{1,3},{2,0},{3,1},{4,6},{5,7},{6,4},{7,5},{8,10},{9,11},{10,... | collective-permute-start | bytes 491528 | tf_op jit(solution)/shard_map/ppermute | solution.py:275
  36.8 10.7 %collective-permute-start.10 = (bf16[40,8,256]{2,1,0:T(8,128)(2,1)S(1)}, bf16[40,8,256]{2,1,0:T(8,128)(2,1)S(1)}, u32[]{:S(2)}, u32[]{:S(2)}) collective-permute-start(bf16[40,8,256]{2,1,0:T(8,128)(2,1)S(1)} %collective-permute-done.2.rest_refs_3_), channel_id=1, source_target_pairs={{0,1},{1,0},{2,3},{3,2},{4,5},{5,4},{6,7},{7,6},{8,9},{9,8},{10,11... | collective-permute-start | bytes 491528 | tf_op jit(solution)/shard_map/ppermute | solution.py:275
  39.3 8.3 %collective-permute-start.11 = (bf16[40,8,256]{2,1,0:T(8,128)(2,1)S(1)}, bf16[40,8,256]{2,1,0:T(8,128)(2,1)S(1)}, u32[]{:S(2)}, u32[]{:S(2)}) collective-permute-start(bf16[40,8,256]{2,1,0:T(8,128)(2,1)S(1)} %collective-permute-done.3.rest_refs_4_), channel_id=1, source_target_pairs={{0,1},{1,0},{2,3},{3,2},{4,5},{5,4},{6,7},{7,6},{8,9},{9,8},{10,11... | collective-permute-start | bytes 491528 | tf_op jit(solution)/shard_map/ppermute | solution.py:275
  39.3 8.3 %collective-permute-start.12 = (bf16[40,8,256]{2,1,0:T(8,128)(2,1)S(1)}, bf16[40,8,256]{2,1,0:T(8,128)(2,1)S(1)}, u32[]{:S(2)}, u32[]{:S(2)}) collective-permute-start(bf16[40,8,256]{2,1,0:T(8,128)(2,1)S(1)} %collective-permute-done.4.rest_refs_5_), channel_id=1, source_target_pairs={{0,1},{1,0},{2,3},{3,2},{4,5},{5,4},{6,7},{7,6},{8,9},{9,8},{10,11... | collective-permute-start | bytes 491528 | tf_op jit(solution)/shard_map/ppermute | solution.py:275
  42.8 4.8 %collective-permute-start.13 = (bf16[40,8,256]{2,1,0:T(8,128)(2,1)S(1)}, bf16[40,8,256]{2,1,0:T(8,128)(2,1)S(1)}, u32[]{:S(2)}, u32[]{:S(2)}) collective-permute-start(bf16[40,8,256]{2,1,0:T(8,128)(2,1)S(1)} %collective-permute-done.5.rest_refs_6_), channel_id=1, source_target_pairs={{0,1},{1,0},{2,3},{3,2},{4,5},{5,4},{6,7},{7,6},{8,9},{9,8},{10,11... | collective-permute-start | bytes 491528 | tf_op jit(solution)/shard_map/ppermute | solution.py:275
  45.5 2.0 %collective-permute-start.14 = (bf16[40,8,256]{2,1,0:T(8,128)(2,1)S(1)}, bf16[40,8,256]{2,1,0:T(8,128)(2,1)S(1)}, u32[]{:S(2)}, u32[]{:S(2)}) collective-permute-start(bf16[40,8,256]{2,1,0:T(8,128)(2,1)S(1)} %collective-permute-done.6.rest_refs_7_), channel_id=1, source_target_pairs={{0,1},{1,0},{2,3},{3,2},{4,5},{5,4},{6,7},{7,6},{8,9},{9,8},{10,11... | collective-permute-start | bytes 491528 | tf_op jit(solution)/shard_map/ppermute | solution.py:275
  45.5 0.9 %copy-start.1 = (bf16[40,8,256]{2,1,0:T(8,128)(2,1)S(1)}, bf16[40,8,256]{2,1,0:T(8,128)(2,1)}, u32[]{:S(2)}) copy-start(bf16[40,8,256]{2,1,0:T(8,128)(2,1)} %get-tuple-element.10.own_ref) | copy-start | bytes 491524

commit v3 on v2

--- a/solution.py
+++ b/solution.py
@@ -281,7 +281,10 @@
     ]
     for axis, stride in ((inner // core, core), (core, 1)):
         pieces = pieces + [
-            move(piece, lambda d, k=shift: d + ((d // stride + k) % axis - d // stride % axis) * stride)
+            move(
+                piece,
+                lambda d, k=shift: d + ((d // stride + k) % axis - d // stride % axis) * stride,
+            )
             for shift in range(1, axis)
             for piece in pieces
         ]
@@ -311,91 +314,56 @@
     )(weight, own)
 
 
-def pair_kernel(count, halves, inner, weight_ref, bias_ref, *rest_refs):
-    pieces = len(rest_refs) - 6
+def pair_kernel(inner, blocks, weight_ref, bias_ref, *rest_refs):
+    pieces = len(rest_refs) - 5
     piece_refs = rest_refs[:pieces]
-    out_ref, right_scr, left_scr, flat_scr, outer_scr, sems = rest_refs[pieces:]
-    groups, depth, residues = right_scr.shape
-    height = halves * count
-    width = groups * halves
-    block = out_ref.shape[0]
-    half = flat_scr.shape[1] // halves
-    slabs = left_scr.shape[0]
-
-    @pl.when(pl.program_id(0) == 0)
-    def prepare():
-        mine = lax.rem(lax.axis_index("wide"), inner) * slabs + groups
-        copies = []
-        for number, piece_ref in enumerate(piece_refs):
-            rows = pl.ds(number * height, height)
-            copies.append(
-                pltpu.make_async_copy(
-                    piece_ref.at[pl.ds(mine, slabs)], left_scr.at[:, rows], sems.at[0, number]
-                )
-            )
-            copies.append(
-                pltpu.make_async_copy(
-                    piece_ref.at[pl.ds(0, groups)], right_scr.at[:, rows], sems.at[1, number]
-                )
-            )
-        for copy in copies:
-            copy.start()
-        for copy in copies[0::2]:
-            copy.wait()
-        left = jnp.concatenate([left_scr[slab] for slab in range(slabs)], axis=1)[:, 0:half].astype(F32)
-        member = lax.broadcasted_iota(jnp.int32, (depth, 1), 0) % height // count
-        for e in range(halves):
-            for h in range(halves):
-                moved = left
-                if e != h:
-                    moved = pltpu.roll(left.reshape(pieces, height, half), (e - h) % halves * count, 1)
-                    moved = moved.reshape(depth, half)
-                moved = jnp.where(member == e, moved, 0.0)
-                flat_scr[e, h * half : (h + 1) * half, :] = moved.T.astype(BF16)
-        for copy in copies[1::2]:
-            copy.wait()
-
-    rows = block * width
-    start = pl.multiple_of(pl.program_id(0) * rows, rows)
-    for group in range(groups):
-        for e in range(halves):
-            product = dot(flat_scr[e, pl.ds(start, rows), :], right_scr[group], ((1,), (0,))).astype(BF16)
-            place = (group * halves + e) * width
-            outer_scr[:, place : place + width, :] = product.reshape(block, width, residues)
+    out_hbm, flat_scr, outer_scr, out_scr, sems = rest_refs[pieces:]
+    slabs, count, residues = piece_refs[0].shape
+    block, depth = out_scr.shape[1], outer_scr.shape[1]
+    width = round(depth**0.5)
+    slabs = (slabs - width) // inner
+    mine = lax.rem(lax.axis_index("wide"), inner) * slabs + width
+    for slab in range(slabs):
+        left = jnp.concatenate([ref[mine + slab].astype(F32) for ref in piece_refs], axis=0)
+        flat_scr[slab * residues : (slab + 1) * residues, :] = left.T.astype(BF16)
     total = float(pieces * count)
-    for i in range(block):
-        projected = dot(weight_ref[...], outer_scr[i], ((1,), (0,)))
-        out_ref[i] = projected.T * (1.0 / total) + bias_ref[...]
+    copies = [
+        pltpu.make_async_copy(out_scr.at[n], out_hbm.at[pl.ds(n * block, block)], sems.at[n])
+        for n in range(blocks)
+    ]
+    for n in range(blocks):
+        rows = slice(n * block * width, (n + 1) * block * width)
+        for e in range(width):
+            right = jnp.concatenate([ref[e].astype(F32) for ref in piece_refs], axis=0).astype(BF16)
+            product = dot(flat_scr[rows, :], right, ((1,), (0,))).astype(BF16)
+            outer_scr[:, e * width : (e + 1) * width, :] = product.reshape(block, width, residues)
+        for i in range(block):
+            projected = dot(weight_ref[...], outer_scr[i], ((1,), (0,)))
+            out_scr[n, i] = projected.T * (1.0 / total) + bias_ref[...]
+        copies[n].start()
+    for copy in copies:
+        copy.wait()
 
 
 def pair_features(pieces, weight, bias, count, inner, owned, blocks):
-    slabs, height, residues = pieces[0].shape
-    halves = height // count
+    residues = pieces[0].shape[2]
+    channels = weight.shape[0]
     width = round(weight.shape[1] ** 0.5)
-    groups = width // halves
-    slabs = (slabs - groups) // inner
-    depth = len(pieces) * height
-    channels = weight.shape[0]
     block = owned // blocks
     scratch = [
-        ((groups, depth, residues), BF16),
-        ((slabs, depth, residues), BF16),
-        ((halves, owned * width, depth), BF16),
+        ((owned * width, len(pieces) * count), BF16),
         ((block, width * width, residues), BF16),
+        ((blocks, block, residues, channels), F32),
     ]
-    used = room(scratch) + 2 * room([(weight.shape, BF16), ((block, residues, channels), F32)])
+    used = room(scratch) + 2 * room([(weight.shape, BF16)])
+    vmem = pl.BlockSpec(memory_space=pltpu.VMEM)
     return pl.pallas_call(
-        functools.partial(pair_kernel, count, halves, inner),
-        grid=(blocks,),
-        in_specs=[
-            pl.BlockSpec(weight.shape, lambda i: (0, 0)),
-            pl.BlockSpec((1, channels), lambda i: (0, 0)),
-        ]
-        + [pl.BlockSpec(memory_space=pl.ANY)] * len(pieces),
-        out_specs=pl.BlockSpec((block, residues, channels), lambda i: (i, 0, 0)),
+        functools.partial(pair_kernel, inner, blocks),
+        in_specs=[vmem] * (2 + len(pieces)),
+        out_specs=pl.BlockSpec(memory_space=pl.ANY),
         out_shape=jax.ShapeDtypeStruct((owned, residues, channels), F32),
         scratch_shapes=[pltpu.VMEM(shape, dtype) for shape, dtype in scratch]
-        + [pltpu.SemaphoreType.DMA((2, len(pieces)))],
+        + [pltpu.SemaphoreType.DMA((blocks,))],
         compiler_params=pltpu.CompilerParams(vmem_limit_bytes=used + 12 * 2**20),
         name="pair",
     )(weight, bias.reshape(1, -1), *pieces)

time: 53.4 us -> 52.4 us (0.981)
  Pallas kernels: 20.9 us -> 19.9 us
    pallas_call x1, Pallas kernels: 5.59 us -> 4.64 us  [pair_features(): pl.pallas_call(functools.partial(pair_kernel, inner, blocks), in_specs=[v...]
where the time goes in v3:
time: 52.4 us; the launch traced here: 52.2 us
  Pallas kernels  19.9 us (38%)
  waiting for transfers between devices  19.1 us (36%)
  starting transfers between devices  11.6 us (22%)
  local copies, waits for them, and re-layouts  0.92 us (2%)
  between operations  0.73 us (1%)
    ppermute x15, waiting for transfers between devices, move(): return lax.ppermute(piece, 'wide', [(d, target(d)) for d in range(devices)])  19.1 us
    pallas_call x1, Pallas kernels, attention(): pl.pallas_call(functools.partial(attention_kernel, heads, owners, outer,...  14.2 us
    ppermute x15, starting transfers between devices, move(): return lax.ppermute(piece, 'wide', [(d, target(d)) for d in range(devices)])  11.6 us
    pallas_call x1, Pallas kernels, pair_features(): pl.pallas_call(functools.partial(pair_kernel, inner, blocks), in_specs=[v...  4.64 us
    pallas_call x1, Pallas kernels, ordered(): pl.pallas_call(order_kernel, in_specs=[pl.BlockSpec(weight.shape, lambda:...  1.07 us
  transfers between devices with their start and end apart: 15, of which 5 were waited for; matrix products, arithmetic and copies ran while one was open for 0% of the time, Pallas kernels for 2%

profile of v3, /device:TPU:0, one launch (start us, length us, event | category | flops | bytes accessed | tf_op | source)
XLA Modules:
  0.0 52.2 jit_solution(6579238993428918109)
XLA Ops:
  0.7 14.2 %attention.1 = (f32[8,256,256]{2,1,0:T(8,128)}, bf16[40,8,256]{2,1,0:T(8,128)(2,1)}, bf16[40,8,256]{2,1,0:T(8,128)(2,1)}, bf16[40,8,256]{2,1,0:T(8,128)(2,1)}, bf16[40,8,256]{2,1,0:T(8,128)(2,1)}) custom-call(s32[8,256]{1,0:T(8,128)} %refs_0_.1, s32[1,256]{1,0:T(1,128)} %bitcast.12, f32[256,256]{1,0:T(8,128)} %refs_2_.1, f32[23,256]{1,0:T(8,128)} %refs_3_.1, ...), custom_call_target="tpu_custom_call" | custom-call | flops 5368709120 | bytes 2097152 | tf_op jit(solution)/shard_map/attention/pallas_call | solution.py:252
  14.9 3.1 %collective-permute-start = (bf16[40,8,256]{2,1,0:T(8,128)(2,1)}, bf16[40,8,256]{2,1,0:T(8,128)(2,1)S(1)}, u32[]{:S(2)}, u32[]{:S(2)}) collective-permute-start(bf16[40,8,256]{2,1,0:T(8,128)(2,1)} %get-tuple-element.13), channel_id=1, source_target_pairs={{0,4},{1,5},{2,6},{3,7},{4,0},{5,1},{6,2},{7,3},{8,12},{9,13},{10,... | collective-permute-start | bytes 491528 | tf_op jit(solution)/shard_map/ppermute | solution.py:275
  18.0 2.6 %collective-permute-start.1 = (bf16[40,8,256]{2,1,0:T(8,128)(2,1)}, bf16[40,8,256]{2,1,0:T(8,128)(2,1)S(1)}, u32[]{:S(2)}, u32[]{:S(2)}) collective-permute-start(bf16[40,8,256]{2,1,0:T(8,128)(2,1)} %get-tuple-element.14), channel_id=1, source_target_pairs={{0,8},{1,9},{2,10},{3,11},{4,12},{5,13},{6,14},{7,15},{8,0},{9,1},... | collective-permute-start | bytes 491528 | tf_op jit(solution)/shard_map/ppermute | solution.py:275
  20.6 0.0 collective-permute-start.7
  20.6 1.7 %collective-permute-start.3 = (bf16[40,8,256]{2,1,0:T(8,128)(2,1)}, bf16[40,8,256]{2,1,0:T(8,128)(2,1)S(1)}, u32[]{:S(2)}, u32[]{:S(2)}) collective-permute-start(bf16[40,8,256]{2,1,0:T(8,128)(2,1)} %get-tuple-element.10.own_ref), channel_id=1, source_target_pairs={{0,2},{1,3},{2,0},{3,1},{4,6},{5,7},{6,4},{7,5},{8,10},{9,11},{10,... | collective-permute-start | bytes 491528 | tf_op jit(solution)/shard_map/ppermute | solution.py:275
  22.3 2.6 %collective-permute-done.rest_refs_1_ = bf16[40,8,256]{2,1,0:T(8,128)(2,1)S(1)} collective-permute-done((bf16[40,8,256]{2,1,0:T(8,128)(2,1)}, bf16[40,8,256]{2,1,0:T(8,128)(2,1)S(1)}, u32[]{:S(2)}, u32[]{:S(2)}) %collective-permute-start) | collective-permute-done | bytes 163872 | tf_op jit(solution)/shard_map/ppermute | solution.py:275
  24.9 0.0 collective-permute-start.8
  24.9 8.3 %collective-permute-done.1.rest_refs_2_ = bf16[40,8,256]{2,1,0:T(8,128)(2,1)S(1)} collective-permute-done((bf16[40,8,256]{2,1,0:T(8,128)(2,1)}, bf16[40,8,256]{2,1,0:T(8,128)(2,1)S(1)}, u32[]{:S(2)}, u32[]{:S(2)}) %collective-permute-start.1) | collective-permute-done | bytes 163872 | tf_op jit(solution)/shard_map/ppermute | solution.py:275
  33.2 1.5 %collective-permute-start.4 = (bf16[40,8,256]{2,1,0:T(8,128)(2,1)S(1)}, bf16[40,8,256]{2,1,0:T(8,128)(2,1)S(1)}, u32[]{:S(2)}, u32[]{:S(2)}) collective-permute-start(bf16[40,8,256]{2,1,0:T(8,128)(2,1)S(1)} %collective-permute-done.rest_refs_1_), channel_id=1, source_target_pairs={{0,2},{1,3},{2,0},{3,1},{4,6},{5,7},{6,4},{7,5},{8,10},{9,11},{10,... | collective-permute-start | bytes 491528 | tf_op jit(solution)/shard_map/ppermute | solution.py:275
  34.7 0.0 collective-permute-done.2.rest_refs_3_
  34.7 0.0 collective-permute-start.9
  34.7 0.0 collective-permute-done.7.rest_refs_8_
  34.7 0.6 %collective-permute-start.5 = (bf16[40,8,256]{2,1,0:T(8,128)(2,1)S(1)}, bf16[40,8,256]{2,1,0:T(8,128)(2,1)S(1)}, u32[]{:S(2)}, u32[]{:S(2)}) collective-permute-start(bf16[40,8,256]{2,1,0:T(8,128)(2,1)S(1)} %collective-permute-done.1.rest_refs_2_), channel_id=1, source_target_pairs={{0,2},{1,3},{2,0},{3,1},{4,6},{5,7},{6,4},{7,5},{8,10},{9,11},{10,... | collective-permute-start | bytes 491528 | tf_op jit(solution)/shard_map/ppermute | solution.py:275
  35.3 1.5 %collective-permute-start.6 = (bf16[40,8,256]{2,1,0:T(8,128)(2,1)S(1)}, bf16[40,8,256]{2,1,0:T(8,128)(2,1)S(1)}, u32[]{:S(2)}, u32[]{:S(2)}) collective-permute-start(bf16[40,8,256]{2,1,0:T(8,128)(2,1)S(1)} %collective-permute-done.2.rest_refs_3_), channel_id=1, source_target_pairs={{0,2},{1,3},{2,0},{3,1},{4,6},{5,7},{6,4},{7,5},{8,10},{9,11},{10,... | collective-permute-start | bytes 491528 | tf_op jit(solution)/shard_map/ppermute | solution.py:275
  36.8 0.0 collective-permute-done.8.rest_refs_9_
  36.8 2.4 %collective-permute-done.4.rest_refs_5_ = bf16[40,8,256]{2,1,0:T(8,128)(2,1)S(1)} collective-permute-done((bf16[40,8,256]{2,1,0:T(8,128)(2,1)S(1)}, bf16[40,8,256]{2,1,0:T(8,128)(2,1)S(1)}, u32[]{:S(2)}, u32[]{:S(2)}) %collective-permute-start.4) | collective-permute-done | bytes 163872 | tf_op jit(solution)/shard_map/ppermute | solution.py:275
  39.3 0.0 collective-permute-start.11
  39.3 0.0 collective-permute-done.9.rest_refs_10_
  39.3 0.5 collective-permute-start.12
  39.8 3.0 %collective-permute-done.5.rest_refs_6_ = bf16[40,8,256]{2,1,0:T(8,128)(2,1)S(1)} collective-permute-done((bf16[40,8,256]{2,1,0:T(8,128)(2,1)S(1)}, bf16[40,8,256]{2,1,0:T(8,128)(2,1)S(1)}, u32[]{:S(2)}, u32[]{:S(2)}) %collective-permute-start.5) | collective-permute-done | bytes 163872 | tf_op jit(solution)/shard_map/ppermute | solution.py:275
  42.8 2.8 %collective-permute-done.6.rest_refs_7_ = bf16[40,8,256]{2,1,0:T(8,128)(2,1)S(1)} collective-permute-done((bf16[40,8,256]{2,1,0:T(8,128)(2,1)S(1)}, bf16[40,8,256]{2,1,0:T(8,128)(2,1)S(1)}, u32[]{:S(2)}, u32[]{:S(2)}) %collective-permute-start.6) | collective-permute-done | bytes 163872 | tf_op jit(solution)/shard_map/ppermute | solution.py:275
  45.6 0.9 %copy-done.1 = bf16[40,8,256]{2,1,0:T(8,128)(2,1)S(1)} copy-done((bf16[40,8,256]{2,1,0:T(8,128)(2,1)S(1)}, bf16[40,8,256]{2,1,0:T(8,128)(2,1)}, u32[]{:S(2)}) %copy-start.1) | copy-done | bytes 163864
  46.5 1.1 %order.1 = (bf16[128,1024]{1,0:T(8,128)(2,1)S(1)}, bf16[40,8,256]{2,1,0:T(8,128)(2,1)S(1)}) custom-call(bf16[1024,128]{1,0:T(8,128)(2,1)S(1)} %copy-done, bf16[40,8,256]{2,1,0:T(8,128)(2,1)S(1)} %copy-done.1), custom_call_target="tpu_custom_call" | custom-call | bytes 524288 | tf_op jit(solution)/shard_map/order/pallas_call | solution.py:306
  47.6 4.6 %pair.1 = f32[16,256,128]{2,1,0:T(8,128)} custom-call(bf16[128,1024]{1,0:T(8,128)(2,1)S(1)} %get-tuple-element.11.weight_ref, f32[1,128]{1,0:T(1,128)S(1)} %bitcast.8, bf16[40,8,256]{2,1,0:T(8,128)(2,1)S(1)} %get-tuple-element.12.rest_refs_0_, bf16[40,8,256]{2,1,0:T(8,128)(2,1)S(1)} %collective-permute-done.rest_refs_1_, ...), custom_call_target="tpu_custom_call" | custom-call | tf_op jit(solution)/shard_map/pair/pallas_call | solution.py:360
  (15 shorter events, 0.0 us)
Async XLA Ops:
  0.6 44.9 %copy-start = (bf16[1024,128]{1,0:T(8,128)(2,1)S(1)}, bf16[1024,128]{1,0:T(8,128)(2,1)}, u32[]{:S(2)}) copy-start(bf16[1024,128]{1,0:T(8,128)(2,1)} %weight_ref.1) | copy-start | bytes 786436
  0.6 47.0 %copy-start.2 = (f32[128]{0:T(128)S(1)}, f32[128]{0:T(128)}, u32[]{:S(2)}) copy-start(f32[128]{0:T(128)} %param.33) | copy-start | bytes 1540
  14.9 10.0 %collective-permute-start = (bf16[40,8,256]{2,1,0:T(8,128)(2,1)}, bf16[40,8,256]{2,1,0:T(8,128)(2,1)S(1)}, u32[]{:S(2)}, u32[]{:S(2)}) collective-permute-start(bf16[40,8,256]{2,1,0:T(8,128)(2,1)} %get-tuple-element.13), channel_id=1, source_target_pairs={{0,4},{1,5},{2,6},{3,7},{4,0},{5,1},{6,2},{7,3},{8,12},{9,13},{10,... | collective-permute-start | bytes 491528 | tf_op jit(solution)/shard_map/ppermute | solution.py:275
  18.0 15.2 %collective-permute-start.1 = (bf16[40,8,256]{2,1,0:T(8,128)(2,1)}, bf16[40,8,256]{2,1,0:T(8,128)(2,1)S(1)}, u32[]{:S(2)}, u32[]{:S(2)}) collective-permute-start(bf16[40,8,256]{2,1,0:T(8,128)(2,1)} %get-tuple-element.14), channel_id=1, source_target_pairs={{0,8},{1,9},{2,10},{3,11},{4,12},{5,13},{6,14},{7,15},{8,0},{9,1},... | collective-permute-start | bytes 491528 | tf_op jit(solution)/shard_map/ppermute | solution.py:275
  20.6 14.1 %collective-permute-start.2 = (bf16[40,8,256]{2,1,0:T(8,128)(2,1)}, bf16[40,8,256]{2,1,0:T(8,128)(2,1)S(1)}, u32[]{:S(2)}, u32[]{:S(2)}) collective-permute-start(bf16[40,8,256]{2,1,0:T(8,128)(2,1)} %get-tuple-element.15), channel_id=1, source_target_pairs={{0,12},{1,13},{2,14},{3,15},{4,8},{5,9},{6,10},{7,11},{8,4},{9,5},... | collective-permute-start | bytes 491528 | tf_op jit(solution)/shard_map/ppermute | solution.py:275
  20.6 14.1 %collective-permute-start.7 = (bf16[40,8,256]{2,1,0:T(8,128)(2,1)}, bf16[40,8,256]{2,1,0:T(8,128)(2,1)S(1)}, u32[]{:S(2)}, u32[]{:S(2)}) collective-permute-start(bf16[40,8,256]{2,1,0:T(8,128)(2,1)} %get-tuple-element.10.own_ref), channel_id=1, source_target_pairs={{0,1},{1,0},{2,3},{3,2},{4,5},{5,4},{6,7},{7,6},{8,9},{9,8},{10,11... | collective-permute-start | bytes 491528 | tf_op jit(solution)/shard_map/ppermute | solution.py:275
  20.6 14.7 %collective-permute-start.3 = (bf16[40,8,256]{2,1,0:T(8,128)(2,1)}, bf16[40,8,256]{2,1,0:T(8,128)(2,1)S(1)}, u32[]{:S(2)}, u32[]{:S(2)}) collective-permute-start(bf16[40,8,256]{2,1,0:T(8,128)(2,1)} %get-tuple-element.10.own_ref), channel_id=1, source_target_pairs={{0,2},{1,3},{2,0},{3,1},{4,6},{5,7},{6,4},{7,5},{8,10},{9,11},{10,... | collective-permute-start | bytes 491528 | tf_op jit(solution)/shard_map/ppermute | solution.py:275
  24.9 11.9 %collective-permute-start.8 = (bf16[40,8,256]{2,1,0:T(8,128)(2,1)S(1)}, bf16[40,8,256]{2,1,0:T(8,128)(2,1)S(1)}, u32[]{:S(2)}, u32[]{:S(2)}) collective-permute-start(bf16[40,8,256]{2,1,0:T(8,128)(2,1)S(1)} %collective-permute-done.rest_refs_1_), channel_id=1, source_target_pairs={{0,1},{1,0},{2,3},{3,2},{4,5},{5,4},{6,7},{7,6},{8,9},{9,8},{10,11... | collective-permute-start | bytes 491528 | tf_op jit(solution)/shard_map/ppermute | solution.py:275
  33.2 6.1 %collective-permute-start.4 = (bf16[40,8,256]{2,1,0:T(8,128)(2,1)S(1)}, bf16[40,8,256]{2,1,0:T(8,128)(2,1)S(1)}, u32[]{:S(2)}, u32[]{:S(2)}) collective-permute-start(bf16[40,8,256]{2,1,0:T(8,128)(2,1)S(1)} %collective-permute-done.rest_refs_1_), channel_id=1, source_target_pairs={{0,2},{1,3},{2,0},{3,1},{4,6},{5,7},{6,4},{7,5},{8,10},{9,11},{10,... | collective-permute-start | bytes 491528 | tf_op jit(solution)/shard_map/ppermute | solution.py:275
  34.7 4.5 %collective-permute-start.9 = (bf16[40,8,256]{2,1,0:T(8,128)(2,1)S(1)}, bf16[40,8,256]{2,1,0:T(8,128)(2,1)S(1)}, u32[]{:S(2)}, u32[]{:S(2)}) collective-permute-start(bf16[40,8,256]{2,1,0:T(8,128)(2,1)S(1)} %collective-permute-done.1.rest_refs_2_), channel_id=1, source_target_pairs={{0,1},{1,0},{2,3},{3,2},{4,5},{5,4},{6,7},{7,6},{8,9},{9,8},{10,11... | collective-permute-start | bytes 491528 | tf_op jit(solution)/shard_map/ppermute | solution.py:275
  34.7 8.0 %collective-permute-start.5 = (bf16[40,8,256]{2,1,0:T(8,128)(2,1)S(1)}, bf16[40,8,256]{2,1,0:T(8,128)(2,1)S(1)}, u32[]{:S(2)}, u32[]{:S(2)}) collective-permute-start(bf16[40,8,256]{2,1,0:T(8,128)(2,1)S(1)} %collective-permute-done.1.rest_refs_2_), channel_id=1, source_target_pairs={{0,2},{1,3},{2,0},{3,1},{4,6},{5,7},{6,4},{7,5},{8,10},{9,11},{10,... | collective-permute-start | bytes 491528 | tf_op jit(solution)/shard_map/ppermute | solution.py:275
  35.3 10.2 %collective-permute-start.6 = (bf16[40,8,256]{2,1,0:T(8,128)(2,1)S(1)}, bf16[40,8,256]{2,1,0:T(8,128)(2,1)S(1)}, u32[]{:S(2)}, u32[]{:S(2)}) collective-permute-start(bf16[40,8,256]{2,1,0:T(8,128)(2,1)S(1)} %collective-permute-done.2.rest_refs_3_), channel_id=1, source_target_pairs={{0,2},{1,3},{2,0},{3,1},{4,6},{5,7},{6,4},{7,5},{8,10},{9,11},{10,... | collective-permute-start | bytes 491528 | tf_op jit(solution)/shard_map/ppermute | solution.py:275
  36.8 10.7 %collective-permute-start.10 = (bf16[40,8,256]{2,1,0:T(8,128)(2,1)S(1)}, bf16[40,8,256]{2,1,0:T(8,128)(2,1)S(1)}, u32[]{:S(2)}, u32[]{:S(2)}) collective-permute-start(bf16[40,8,256]{2,1,0:T(8,128)(2,1)S(1)} %collective-permute-done.2.rest_refs_3_), channel_id=1, source_target_pairs={{0,1},{1,0},{2,3},{3,2},{4,5},{5,4},{6,7},{7,6},{8,9},{9,8},{10,11... | collective-permute-start | bytes 491528 | tf_op jit(solution)/shard_map/ppermute | solution.py:275
  39.3 8.3 %collective-permute-start.11 = (bf16[40,8,256]{2,1,0:T(8,128)(2,1)S(1)}, bf16[40,8,256]{2,1,0:T(8,128)(2,1)S(1)}, u32[]{:S(2)}, u32[]{:S(2)}) collective-permute-start(bf16[40,8,256]{2,1,0:T(8,128)(2,1)S(1)} %collective-permute-done.3.rest_refs_4_), channel_id=1, source_target_pairs={{0,1},{1,0},{2,3},{3,2},{4,5},{5,4},{6,7},{7,6},{8,9},{9,8},{10,11... | collective-permute-start | bytes 491528 | tf_op jit(solution)/shard_map/ppermute | solution.py:275
  39.3 8.3 %collective-permute-start.12 = (bf16[40,8,256]{2,1,0:T(8,128)(2,1)S(1)}, bf16[40,8,256]{2,1,0:T(8,128)(2,1)S(1)}, u32[]{:S(2)}, u32[]{:S(2)}) collective-permute-start(bf16[40,8,256]{2,1,0:T(8,128)(2,1)S(1)} %collective-permute-done.4.rest_refs_5_), channel_id=1, source_target_pairs={{0,1},{1,0},{2,3},{3,2},{4,5},{5,4},{6,7},{7,6},{8,9},{9,8},{10,11... | collective-permute-start | bytes 491528 | tf_op jit(solution)/shard_map/ppermute | solution.py:275
  42.8 4.8 %collective-permute-start.13 = (bf16[40,8,256]{2,1,0:T(8,128)(2,1)S(1)}, bf16[40,8,256]{2,1,0:T(8,128)(2,1)S(1)}, u32[]{:S(2)}, u32[]{:S(2)}) collective-permute-start(bf16[40,8,256]{2,1,0:T(8,128)(2,1)S(1)} %collective-permute-done.5.rest_refs_6_), channel_id=1, source_target_pairs={{0,1},{1,0},{2,3},{3,2},{4,5},{5,4},{6,7},{7,6},{8,9},{9,8},{10,11... | collective-permute-start | bytes 491528 | tf_op jit(solution)/shard_map/ppermute | solution.py:275
  45.5 2.0 %collective-permute-start.14 = (bf16[40,8,256]{2,1,0:T(8,128)(2,1)S(1)}, bf16[40,8,256]{2,1,0:T(8,128)(2,1)S(1)}, u32[]{:S(2)}, u32[]{:S(2)}) collective-permute-start(bf16[40,8,256]{2,1,0:T(8,128)(2,1)S(1)} %collective-permute-done.6.rest_refs_7_), channel_id=1, source_target_pairs={{0,1},{1,0},{2,3},{3,2},{4,5},{5,4},{6,7},{7,6},{8,9},{9,8},{10,11... | collective-permute-start | bytes 491528 | tf_op jit(solution)/shard_map/ppermute | solution.py:275
  45.5 0.9 %copy-start.1 = (bf16[40,8,256]{2,1,0:T(8,128)(2,1)S(1)}, bf16[40,8,256]{2,1,0:T(8,128)(2,1)}, u32[]{:S(2)}) copy-start(bf16[40,8,256]{2,1,0:T(8,128)(2,1)} %get-tuple-element.10.own_ref) | copy-start | bytes 491524

commit v4 on v3

--- a/solution.py
+++ b/solution.py
@@ -49,15 +49,15 @@
     (
         tokens_ref,
         offsets_ref,
-        target_ref,
+        target_hbm,
         embed_ref,
         gain_ref,
-        query_ref,
-        key_ref,
-        value_ref,
-        gate_ref,
+        query_hbm,
+        key_hbm,
+        value_hbm,
+        gate_hbm,
         gate_bias_ref,
-        output_ref,
+        output_hbm,
         relative_ref,
         gain_two_ref,
         left_ref,
@@ -77,7 +77,23 @@
         gather_scr,
         narrow_scr,
         sorted_scr,
+        target_ref,
+        query_ref,
+        key_ref,
+        value_ref,
+        gate_ref,
+        output_ref,
+        sems,
     ) = rest_refs[outer:]
+    moved = (
+        (target_hbm, target_ref),
+        (query_hbm, query_ref),
+        (key_hbm, key_ref),
+        (value_hbm, value_ref),
+        (gate_hbm, gate_ref),
+        (output_hbm, output_ref),
+    )
+    copies = [pltpu.make_async_copy(a, b, sems.at[n]) for n, (a, b) in enumerate(moved)]
     step = pl.program_id(0)
     residues, features = target_ref.shape
     head_size = query_ref.shape[1] // heads
@@ -88,12 +104,15 @@
     width = right_ref.shape[0]
     bins = relative_ref.shape[1]
     inner = owners // outer
+    core = 2 if inner % 2 == 0 else 1
     owned = residues // owners
     count = factor_scr.shape[1] // width
     slabs = owned * width // residues
 
     @pl.when(step == 0)
     def prepare():
+        for copy in copies:
+            copy.start()
         relative_scr[...] = jnp.zeros_like(relative_scr)
         relative_scr[0:heads, 0:bins] = relative_ref[...]
         table = relative_scr[...]
@@ -140,6 +159,8 @@
                 mixer_scr[k, member * residues : (member + 1) * residues, LANES:] = jnp.broadcast_to(
                     ones, (residues, LANES)
                 )
+        for copy in copies:
+            copy.wait()
 
     place = lax.broadcasted_iota(jnp.int32, (1, LANES), 1) // head_size
     blank = jnp.zeros((), BF16)
@@ -206,17 +227,21 @@
             owner_scr[tile] = total
         right = jnp.concatenate([factor_scr[t] for t in range(residues // LANES)], axis=1)
         right = right.astype(BF16).reshape(width, count, residues)
-        mine = lax.axis_index("wide") // inner
+        me = lax.axis_index("wide")
+        near = lax.rem(me, inner) // core * core
         per = residues // LANES
+        edge = core * slabs
         for shift, message_ref in enumerate(message_refs):
-            target = meet(mine, shift, outer) * inner
-            message_ref[0:width] = right
+            target = meet(me // inner, shift, outer) * inner
+            message_ref[edge : edge + width] = right
             for k in range(inner):
+                owner = target + lax.rem(near + k, inner)
+                place = k * slabs if k < core else width + k * slabs
                 for slab in range(slabs):
                     block = [
-                        owner_scr[slab * per + t, pl.ds(target + k, count, stride=owners), :] for t in range(per)
+                        owner_scr[slab * per + t, pl.ds(owner, count, stride=owners), :] for t in range(per)
                     ]
-                    message_ref[width + k * slabs + slab] = jnp.concatenate(block, axis=1).astype(BF16)
+                    message_ref[place + slab] = jnp.concatenate(block, axis=1).astype(BF16)
 
 
 def attention(operands, heads, owners, outer):
@@ -249,14 +274,20 @@
         ((count, residues, features), BF16),
         ((owned, count, owners, features), BF16),
     ]
+    moved = (2, 5, 6, 7, 8, 10)
+    in_specs = [
+        pl.BlockSpec(memory_space=pl.ANY) if n in moved else whole(x) for n, x in enumerate(operands)
+    ]
     return pl.pallas_call(
         functools.partial(attention_kernel, heads, owners, outer, together),
         grid=(count // together,),
-        in_specs=[whole(x) for x in operands],
+        in_specs=in_specs,
         out_specs=(pl.BlockSpec((together, residues, features), lambda s: (s, 0, 0)),)
         + tuple(whole(x) for x in outs[1:]),
         out_shape=outs,
-        scratch_shapes=[pltpu.VMEM(shape, dtype) for shape, dtype in scratch],
+        scratch_shapes=[pltpu.VMEM(shape, dtype) for shape, dtype in scratch]
+        + [pltpu.VMEM(operands[n].shape, operands[n].dtype) for n in moved]
+        + [pltpu.SemaphoreType.DMA((len(moved),))],
         cost_estimate=pl.CostEstimate(
             flops=count * residues * (8 * features * features + 8 * heads * residues * LANES),
             transcendentals=count * heads * residues * residues,
@@ -266,7 +297,7 @@
     )(*operands)
 
 
-def spread(messages, devices):
+def spread(messages, devices, edge):
     outer = len(messages)
     inner = devices // outer
     core = 2 if inner % 2 == 0 else 1
@@ -279,10 +310,10 @@
         for shift, message in enumerate(messages)
         if shift
     ]
-    for axis, stride in ((inner // core, core), (core, 1)):
+    for name, axis, stride in (("y", inner // core, core), ("c", core, 1)):
         pieces = pieces + [
             move(
-                piece,
+                piece[edge:] if name == "y" else piece,
                 lambda d, k=shift: d + ((d // stride + k) % axis - d // stride % axis) * stride,
             )
             for shift in range(1, axis)
@@ -321,10 +352,16 @@
     slabs, count, residues = piece_refs[0].shape
     block, depth = out_scr.shape[1], outer_scr.shape[1]
     width = round(depth**0.5)
+    longest = slabs
     slabs = (slabs - width) // inner
-    mine = lax.rem(lax.axis_index("wide"), inner) * slabs + width
+    core = 2 if inner % 2 == 0 else 1
+    mine = lax.rem(lax.axis_index("wide"), core) * slabs
+    starts = [core * slabs if ref.shape[0] == longest else 0 for ref in piece_refs]
+    places = [mine if start else mine + width for start in starts]
     for slab in range(slabs):
-        left = jnp.concatenate([ref[mine + slab].astype(F32) for ref in piece_refs], axis=0)
+        left = jnp.concatenate([
+            ref[place + slab].astype(F32) for ref, place in zip(piece_refs, places)
+        ], axis=0)
         flat_scr[slab * residues : (slab + 1) * residues, :] = left.T.astype(BF16)
     total = float(pieces * count)
     copies = [
@@ -334,7 +371,7 @@
     for n in range(blocks):
         rows = slice(n * block * width, (n + 1) * block * width)
         for e in range(width):
-            right = jnp.concatenate([ref[e].astype(F32) for ref in piece_refs], axis=0).astype(BF16)
+            right = jnp.concatenate([ref[start + e].astype(F32) for ref, start in zip(piece_refs, starts)], axis=0).astype(BF16)
             product = dot(flat_scr[rows, :], right, ((1,), (0,))).astype(BF16)
             outer_scr[:, e * width : (e + 1) * width, :] = product.reshape(block, width, residues)
         for i in range(block):
@@ -410,7 +447,9 @@
     )
     heads = relative_position_table.shape[1]
     updated, *messages = attention(operands, heads, devices, devices // inner)
-    pieces = spread(messages, devices)
+    core = 2 if inner % 2 == 0 else 1
+    edge = core * (residues // devices * left_weight.shape[1] // residues)
+    pieces = spread(messages, devices, edge)
     weight, pieces[0] = ordered(pair_weight, messages[0])
     pair = pair_features(
         pieces,
@@ -419,7 +458,7 @@
         sequences,
         inner,
         residues // devices,
-        2,
+        4,
     )
     return (updated, pair)
 

time: 52.4 us -> 50.2 us (0.958)
  waiting for transfers between devices: 19.1 us -> 14.6 us
  local copies, waits for them, and re-layouts: 0.92 us -> 1.88 us
  starting transfers between devices: 11.6 us -> 12.4 us
    ppermute x15, waiting for transfers between devices: 19.1 us -> 14.6 us  [move(): return lax.ppermute(piece, 'wide', [(d, target(d)) for d in range(devices)])]
    slice x0 -> x4, local copies, waits for them, and re-layouts: none -> 0.95 us  [spread(): piece[edge:]]
    ppermute x15, starting transfers between devices: 11.6 us -> 12.4 us  [move(): return lax.ppermute(piece, 'wide', [(d, target(d)) for d in range(devices)])]
  transfers between devices with their start and end apart: 15 -> 15, of which waited for: 5 -> 4; matrix products, arithmetic and copies ran while one was open for 0% -> 2% of each run, Pallas kernels for 2% -> 2%
where the time goes in v4:
time: 50.2 us; the launch traced here: 50 us
  Pallas kernels  20.4 us (41%)
  waiting for transfers between devices  14.6 us (29%)
  starting transfers between devices  12.4 us (25%)
  local copies, waits for them, and re-layouts  1.88 us (4%)
  between operations  0.76 us (2%)
    pallas_call x1, Pallas kernels, attention(): pl.pallas_call(functools.partial(attention_kernel, heads, owners, outer,...  14.7 us
    ppermute x15, waiting for transfers between devices, move(): return lax.ppermute(piece, 'wide', [(d, target(d)) for d in range(devices)])  14.6 us
    ppermute x15, starting transfers between devices, move(): return lax.ppermute(piece, 'wide', [(d, target(d)) for d in range(devices)])  12.4 us
    pallas_call x1, Pallas kernels, pair_features(): pl.pallas_call(functools.partial(pair_kernel, inner, blocks), in_specs=[v...  4.55 us
    pallas_call x1, Pallas kernels, ordered(): pl.pallas_call(order_kernel, in_specs=[pl.BlockSpec(weight.shape, lambda:...  1.07 us
  transfers between devices with their start and end apart: 15, of which 4 were waited for; matrix products, arithmetic and copies ran while one was open for 2% of the time, Pallas kernels for 2%

profile of v4, /device:TPU:0, one launch (start us, length us, event | category | flops | bytes accessed | tf_op | source)
XLA Modules:
  0.0 50.0 jit_solution(385831263016262901)
XLA Ops:
  0.7 14.7 %attention.1 = (f32[8,256,256]{2,1,0:T(8,128)}, bf16[40,8,256]{2,1,0:T(8,128)(2,1)}, bf16[40,8,256]{2,1,0:T(8,128)(2,1)}, bf16[40,8,256]{2,1,0:T(8,128)(2,1)}, bf16[40,8,256]{2,1,0:T(8,128)(2,1)}) custom-call(s32[8,256]{1,0:T(8,128)} %refs_0_.1, s32[1,256]{1,0:T(1,128)} %bitcast.12, f32[256,256]{1,0:T(8,128)} %refs_2_.1, f32[23,256]{1,0:T(8,128)} %refs_3_.1, ...), custom_call_target="tpu_custom_call" | custom-call | flops 5368709120 | bytes 2097152 | tf_op jit(solution)/shard_map/attention/pallas_call | solution.py:281
  15.4 3.1 %collective-permute-start = (bf16[40,8,256]{2,1,0:T(8,128)(2,1)}, bf16[40,8,256]{2,1,0:T(8,128)(2,1)S(1)}, u32[]{:S(2)}, u32[]{:S(2)}) collective-permute-start(bf16[40,8,256]{2,1,0:T(8,128)(2,1)} %get-tuple-element.13), channel_id=1, source_target_pairs={{0,4},{1,5},{2,6},{3,7},{4,0},{5,1},{6,2},{7,3},{8,12},{9,13},{10,... | collective-permute-start | bytes 491528 | tf_op jit(solution)/shard_map/ppermute | solution.py:306
  18.5 2.6 %collective-permute-start.1 = (bf16[40,8,256]{2,1,0:T(8,128)(2,1)}, bf16[40,8,256]{2,1,0:T(8,128)(2,1)S(1)}, u32[]{:S(2)}, u32[]{:S(2)}) collective-permute-start(bf16[40,8,256]{2,1,0:T(8,128)(2,1)} %get-tuple-element.14), channel_id=1, source_target_pairs={{0,8},{1,9},{2,10},{3,11},{4,12},{5,13},{6,14},{7,15},{8,0},{9,1},... | collective-permute-start | bytes 491528 | tf_op jit(solution)/shard_map/ppermute | solution.py:306
  21.1 0.9 %slice.12 = bf16[36,8,256]{2,1,0:T(8,128)(2,1)S(1)} slice(bf16[40,8,256]{2,1,0:T(8,128)(2,1)} %get-tuple-element.10.own_ref), slice={[4:40], [0:8], [0:256]} | slice | bytes 294912 | tf_op jit(solution)/shard_map/slice | solution.py:316
  22.0 1.6 %collective-permute-start.3 = (bf16[36,8,256]{2,1,0:T(8,128)(2,1)S(1)}, bf16[36,8,256]{2,1,0:T(8,128)(2,1)S(1)}, u32[]{:S(2)}, u32[]{:S(2)}) collective-permute-start(bf16[36,8,256]{2,1,0:T(8,128)(2,1)S(1)} %slice.12), channel_id=1, source_target_pairs={{0,2},{1,3},{2,0},{3,1},{4,6},{5,7},{6,4},{7,5},{8,10},{9,11},{10,... | collective-permute-start | bytes 442376 | tf_op jit(solution)/shard_map/ppermute | solution.py:306
  23.6 0.2 collective-permute-start.2
  23.8 3.4 %collective-permute-done.3.rest_refs_4_ = bf16[36,8,256]{2,1,0:T(8,128)(2,1)S(1)} collective-permute-done((bf16[36,8,256]{2,1,0:T(8,128)(2,1)S(1)}, bf16[36,8,256]{2,1,0:T(8,128)(2,1)S(1)}, u32[]{:S(2)}, u32[]{:S(2)}) %collective-permute-start.3) | collective-permute-done | bytes 147488 | tf_op jit(solution)/shard_map/ppermute | solution.py:306
  27.2 0.0 collective-permute-done.rest_refs_1_
  27.3 1.6 %collective-permute-start.4 = (bf16[36,8,256]{2,1,0:T(8,128)(2,1)S(1)}, bf16[36,8,256]{2,1,0:T(8,128)(2,1)S(1)}, u32[]{:S(2)}, u32[]{:S(2)}) collective-permute-start(bf16[36,8,256]{2,1,0:T(8,128)(2,1)S(1)} %slice.16), channel_id=1, source_target_pairs={{0,2},{1,3},{2,0},{3,1},{4,6},{5,7},{6,4},{7,5},{8,10},{9,11},{10,... | collective-permute-start | bytes 442376 | tf_op jit(solution)/shard_map/ppermute | solution.py:306
  28.8 4.2 %collective-permute-done.1.rest_refs_2_ = bf16[40,8,256]{2,1,0:T(8,128)(2,1)S(1)} collective-permute-done((bf16[40,8,256]{2,1,0:T(8,128)(2,1)}, bf16[40,8,256]{2,1,0:T(8,128)(2,1)S(1)}, u32[]{:S(2)}, u32[]{:S(2)}) %collective-permute-start.1) | collective-permute-done | bytes 163872 | tf_op jit(solution)/shard_map/ppermute | solution.py:306
  33.1 0.0 collective-permute-done.2.rest_refs_3_
  33.1 2.1 %collective-permute-start.5 = (bf16[36,8,256]{2,1,0:T(8,128)(2,1)S(1)}, bf16[36,8,256]{2,1,0:T(8,128)(2,1)S(1)}, u32[]{:S(2)}, u32[]{:S(2)}) collective-permute-start(bf16[36,8,256]{2,1,0:T(8,128)(2,1)S(1)} %slice.17), channel_id=1, source_target_pairs={{0,2},{1,3},{2,0},{3,1},{4,6},{5,7},{6,4},{7,5},{8,10},{9,11},{10,... | collective-permute-start | bytes 442376 | tf_op jit(solution)/shard_map/ppermute | solution.py:306
  35.2 0.0 collective-permute-done.7.rest_refs_8_
  35.2 0.1 collective-permute-start.6
  35.3 0.3 collective-permute-start.9
  35.6 0.3 collective-permute-start.10
  35.9 4.0 %collective-permute-done.5.rest_refs_6_ = bf16[36,8,256]{2,1,0:T(8,128)(2,1)S(1)} collective-permute-done((bf16[36,8,256]{2,1,0:T(8,128)(2,1)S(1)}, bf16[36,8,256]{2,1,0:T(8,128)(2,1)S(1)}, u32[]{:S(2)}, u32[]{:S(2)}) %collective-permute-start.5) | collective-permute-done | bytes 147488 | tf_op jit(solution)/shard_map/ppermute | solution.py:306
  39.9 3.0 %collective-permute-done.6.rest_refs_7_ = bf16[36,8,256]{2,1,0:T(8,128)(2,1)S(1)} collective-permute-done((bf16[36,8,256]{2,1,0:T(8,128)(2,1)S(1)}, bf16[36,8,256]{2,1,0:T(8,128)(2,1)S(1)}, u32[]{:S(2)}, u32[]{:S(2)}) %collective-permute-start.6) | collective-permute-done | bytes 147488 | tf_op jit(solution)/shard_map/ppermute | solution.py:306
  42.8 0.0 collective-permute-start.13
  42.8 0.5 %collective-permute-start.14 = (bf16[36,8,256]{2,1,0:T(8,128)(2,1)S(1)}, bf16[36,8,256]{2,1,0:T(8,128)(2,1)S(1)}, u32[]{:S(2)}, u32[]{:S(2)}) collective-permute-start(bf16[36,8,256]{2,1,0:T(8,128)(2,1)S(1)} %collective-permute-done.6.rest_refs_7_), channel_id=1, source_target_pairs={{0,1},{1,0},{2,3},{3,2},{4,5},{5,4},{6,7},{7,6},{8,9},{9,8},{10,11... | collective-permute-start | bytes 442376 | tf_op jit(solution)/shard_map/ppermute | solution.py:306
  43.4 0.9 %copy-done = bf16[40,8,256]{2,1,0:T(8,128)(2,1)S(1)} copy-done((bf16[40,8,256]{2,1,0:T(8,128)(2,1)S(1)}, bf16[40,8,256]{2,1,0:T(8,128)(2,1)}, u32[]{:S(2)}) %copy-start) | copy-done | bytes 163864
  44.3 1.1 %order.1 = (bf16[128,1024]{1,0:T(8,128)(2,1)S(1)}, bf16[40,8,256]{2,1,0:T(8,128)(2,1)S(1)}) custom-call(bf16[1024,128]{1,0:T(8,128)(2,1)S(1)} %copy-done.1, bf16[40,8,256]{2,1,0:T(8,128)(2,1)S(1)} %copy-done), custom_call_target="tpu_custom_call" | custom-call | bytes 524288 | tf_op jit(solution)/shard_map/order/pallas_call | solution.py:337
  45.4 0.0 collective-permute-done.9.rest_refs_10_
  45.4 4.5 %pair.1 = f32[16,256,128]{2,1,0:T(8,128)} custom-call(bf16[128,1024]{1,0:T(8,128)(2,1)S(1)} %get-tuple-element.11.weight_ref, f32[1,128]{1,0:T(1,128)S(1)} %bitcast.8, bf16[40,8,256]{2,1,0:T(8,128)(2,1)S(1)} %get-tuple-element.12.rest_refs_0_, bf16[40,8,256]{2,1,0:T(8,128)(2,1)S(1)} %collective-permute-done.rest_refs_1_, ...), custom_call_target="tpu_custom_call" | custom-call | tf_op jit(solution)/shard_map/pair/pallas_call | solution.py:397
  (19 shorter events, 0.1 us)
Async XLA Ops:
  0.6 42.7 %copy-start.1 = (bf16[1024,128]{1,0:T(8,128)(2,1)S(1)}, bf16[1024,128]{1,0:T(8,128)(2,1)}, u32[]{:S(2)}) copy-start(bf16[1024,128]{1,0:T(8,128)(2,1)} %weight_ref.1) | copy-start | bytes 786436
  0.6 44.8 %copy-start.2 = (f32[128]{0:T(128)S(1)}, f32[128]{0:T(128)}, u32[]{:S(2)}) copy-start(f32[128]{0:T(128)} %param.33) | copy-start | bytes 1540
  15.4 11.8 %collective-permute-start = (bf16[40,8,256]{2,1,0:T(8,128)(2,1)}, bf16[40,8,256]{2,1,0:T(8,128)(2,1)S(1)}, u32[]{:S(2)}, u32[]{:S(2)}) collective-permute-start(bf16[40,8,256]{2,1,0:T(8,128)(2,1)} %get-tuple-element.13), channel_id=1, source_target_pairs={{0,4},{1,5},{2,6},{3,7},{4,0},{5,1},{6,2},{7,3},{8,12},{9,13},{10,... | collective-permute-start | bytes 491528 | tf_op jit(solution)/shard_map/ppermute | solution.py:306
  18.5 14.5 %collective-permute-start.1 = (bf16[40,8,256]{2,1,0:T(8,128)(2,1)}, bf16[40,8,256]{2,1,0:T(8,128)(2,1)S(1)}, u32[]{:S(2)}, u32[]{:S(2)}) collective-permute-start(bf16[40,8,256]{2,1,0:T(8,128)(2,1)} %get-tuple-element.14), channel_id=1, source_target_pairs={{0,8},{1,9},{2,10},{3,11},{4,12},{5,13},{6,14},{7,15},{8,0},{9,1},... | collective-permute-start | bytes 491528 | tf_op jit(solution)/shard_map/ppermute | solution.py:306
  22.0 5.2 %collective-permute-start.3 = (bf16[36,8,256]{2,1,0:T(8,128)(2,1)S(1)}, bf16[36,8,256]{2,1,0:T(8,128)(2,1)S(1)}, u32[]{:S(2)}, u32[]{:S(2)}) collective-permute-start(bf16[36,8,256]{2,1,0:T(8,128)(2,1)S(1)} %slice.12), channel_id=1, source_target_pairs={{0,2},{1,3},{2,0},{3,1},{4,6},{5,7},{6,4},{7,5},{8,10},{9,11},{10,... | collective-permute-start | bytes 442376 | tf_op jit(solution)/shard_map/ppermute | solution.py:306
  23.6 9.5 %collective-permute-start.2 = (bf16[40,8,256]{2,1,0:T(8,128)(2,1)}, bf16[40,8,256]{2,1,0:T(8,128)(2,1)S(1)}, u32[]{:S(2)}, u32[]{:S(2)}) collective-permute-start(bf16[40,8,256]{2,1,0:T(8,128)(2,1)} %get-tuple-element.15), channel_id=1, source_target_pairs={{0,12},{1,13},{2,14},{3,15},{4,8},{5,9},{6,10},{7,11},{8,4},{9,5},... | collective-permute-start | bytes 491528 | tf_op jit(solution)/shard_map/ppermute | solution.py:306
  23.8 11.3 %collective-permute-start.7 = (bf16[40,8,256]{2,1,0:T(8,128)(2,1)}, bf16[40,8,256]{2,1,0:T(8,128)(2,1)S(1)}, u32[]{:S(2)}, u32[]{:S(2)}) collective-permute-start(bf16[40,8,256]{2,1,0:T(8,128)(2,1)} %get-tuple-element.10.own_ref), channel_id=1, source_target_pairs={{0,1},{1,0},{2,3},{3,2},{4,5},{5,4},{6,7},{7,6},{8,9},{9,8},{10,11... | collective-permute-start | bytes 491528 | tf_op jit(solution)/shard_map/ppermute | solution.py:306
  27.2 8.0 %collective-permute-start.11 = (bf16[36,8,256]{2,1,0:T(8,128)(2,1)S(1)}, bf16[36,8,256]{2,1,0:T(8,128)(2,1)S(1)}, u32[]{:S(2)}, u32[]{:S(2)}) collective-permute-start(bf16[36,8,256]{2,1,0:T(8,128)(2,1)S(1)} %collective-permute-done.3.rest_refs_4_), channel_id=1, source_target_pairs={{0,1},{1,0},{2,3},{3,2},{4,5},{5,4},{6,7},{7,6},{8,9},{9,8},{10,11... | collective-permute-start | bytes 442376 | tf_op jit(solution)/shard_map/ppermute | solution.py:306
  27.3 8.3 %collective-permute-start.4 = (bf16[36,8,256]{2,1,0:T(8,128)(2,1)S(1)}, bf16[36,8,256]{2,1,0:T(8,128)(2,1)S(1)}, u32[]{:S(2)}, u32[]{:S(2)}) collective-permute-start(bf16[36,8,256]{2,1,0:T(8,128)(2,1)S(1)} %slice.16), channel_id=1, source_target_pairs={{0,2},{1,3},{2,0},{3,1},{4,6},{5,7},{6,4},{7,5},{8,10},{9,11},{10,... | collective-permute-start | bytes 442376 | tf_op jit(solution)/shard_map/ppermute | solution.py:306
  33.1 9.8 %collective-permute-start.8 = (bf16[40,8,256]{2,1,0:T(8,128)(2,1)S(1)}, bf16[40,8,256]{2,1,0:T(8,128)(2,1)S(1)}, u32[]{:S(2)}, u32[]{:S(2)}) collective-permute-start(bf16[40,8,256]{2,1,0:T(8,128)(2,1)S(1)} %collective-permute-done.rest_refs_1_), channel_id=1, source_target_pairs={{0,1},{1,0},{2,3},{3,2},{4,5},{5,4},{6,7},{7,6},{8,9},{9,8},{10,11... | collective-permute-start | bytes 491528 | tf_op jit(solution)/shard_map/ppermute | solution.py:306
  33.1 6.8 %collective-permute-start.5 = (bf16[36,8,256]{2,1,0:T(8,128)(2,1)S(1)}, bf16[36,8,256]{2,1,0:T(8,128)(2,1)S(1)}, u32[]{:S(2)}, u32[]{:S(2)}) collective-permute-start(bf16[36,8,256]{2,1,0:T(8,128)(2,1)S(1)} %slice.17), channel_id=1, source_target_pairs={{0,2},{1,3},{2,0},{3,1},{4,6},{5,7},{6,4},{7,5},{8,10},{9,11},{10,... | collective-permute-start | bytes 442376 | tf_op jit(solution)/shard_map/ppermute | solution.py:306
  35.2 7.7 %collective-permute-start.6 = (bf16[36,8,256]{2,1,0:T(8,128)(2,1)S(1)}, bf16[36,8,256]{2,1,0:T(8,128)(2,1)S(1)}, u32[]{:S(2)}, u32[]{:S(2)}) collective-permute-start(bf16[36,8,256]{2,1,0:T(8,128)(2,1)S(1)} %slice.18), channel_id=1, source_target_pairs={{0,2},{1,3},{2,0},{3,1},{4,6},{5,7},{6,4},{7,5},{8,10},{9,11},{10,... | collective-permute-start | bytes 442376 | tf_op jit(solution)/shard_map/ppermute | solution.py:306
  35.3 10.1 %collective-permute-start.9 = (bf16[40,8,256]{2,1,0:T(8,128)(2,1)S(1)}, bf16[40,8,256]{2,1,0:T(8,128)(2,1)S(1)}, u32[]{:S(2)}, u32[]{:S(2)}) collective-permute-start(bf16[40,8,256]{2,1,0:T(8,128)(2,1)S(1)} %collective-permute-done.1.rest_refs_2_), channel_id=1, source_target_pairs={{0,1},{1,0},{2,3},{3,2},{4,5},{5,4},{6,7},{7,6},{8,9},{9,8},{10,11... | collective-permute-start | bytes 491528 | tf_op jit(solution)/shard_map/ppermute | solution.py:306
  35.6 9.8 %collective-permute-start.10 = (bf16[40,8,256]{2,1,0:T(8,128)(2,1)S(1)}, bf16[40,8,256]{2,1,0:T(8,128)(2,1)S(1)}, u32[]{:S(2)}, u32[]{:S(2)}) collective-permute-start(bf16[40,8,256]{2,1,0:T(8,128)(2,1)S(1)} %collective-permute-done.2.rest_refs_3_), channel_id=1, source_target_pairs={{0,1},{1,0},{2,3},{3,2},{4,5},{5,4},{6,7},{7,6},{8,9},{9,8},{10,11... | collective-permute-start | bytes 491528 | tf_op jit(solution)/shard_map/ppermute | solution.py:306
  39.9 5.5 %collective-permute-start.12 = (bf16[36,8,256]{2,1,0:T(8,128)(2,1)S(1)}, bf16[36,8,256]{2,1,0:T(8,128)(2,1)S(1)}, u32[]{:S(2)}, u32[]{:S(2)}) collective-permute-start(bf16[36,8,256]{2,1,0:T(8,128)(2,1)S(1)} %collective-permute-done.4.rest_refs_5_), channel_id=1, source_target_pairs={{0,1},{1,0},{2,3},{3,2},{4,5},{5,4},{6,7},{7,6},{8,9},{9,8},{10,11... | collective-permute-start | bytes 442376 | tf_op jit(solution)/shard_map/ppermute | solution.py:306
  42.8 2.5 %collective-permute-start.13 = (bf16[36,8,256]{2,1,0:T(8,128)(2,1)S(1)}, bf16[36,8,256]{2,1,0:T(8,128)(2,1)S(1)}, u32[]{:S(2)}, u32[]{:S(2)}) collective-permute-start(bf16[36,8,256]{2,1,0:T(8,128)(2,1)S(1)} %collective-permute-done.5.rest_refs_6_), channel_id=1, source_target_pairs={{0,1},{1,0},{2,3},{3,2},{4,5},{5,4},{6,7},{7,6},{8,9},{9,8},{10,11... | collective-permute-start | bytes 442376 | tf_op jit(solution)/shard_map/ppermute | solution.py:306
  42.8 2.6 %collective-permute-start.14 = (bf16[36,8,256]{2,1,0:T(8,128)(2,1)S(1)}, bf16[36,8,256]{2,1,0:T(8,128)(2,1)S(1)}, u32[]{:S(2)}, u32[]{:S(2)}) collective-permute-start(bf16[36,8,256]{2,1,0:T(8,128)(2,1)S(1)} %collective-permute-done.6.rest_refs_7_), channel_id=1, source_target_pairs={{0,1},{1,0},{2,3},{3,2},{4,5},{5,4},{6,7},{7,6},{8,9},{9,8},{10,11... | collective-permute-start | bytes 442376 | tf_op jit(solution)/shard_map/ppermute | solution.py:306
  43.4 0.9 %copy-start = (bf16[40,8,256]{2,1,0:T(8,128)(2,1)S(1)}, bf16[40,8,256]{2,1,0:T(8,128)(2,1)}, u32[]{:S(2)}) copy-start(bf16[40,8,256]{2,1,0:T(8,128)(2,1)} %get-tuple-element.10.own_ref) | copy-start | bytes 491524
